TPU v7x, 512 devices: a whole 4x4x16 slice. The times are simulated.
512 devices in a mesh: ctx: 32 (over z, core), bal: 16 (over x, y).
Axes of the slice: x: 4, y: 4, z: 16, core: 2. Of those that a mesh axis runs over, the one named last changes fastest.
Arguments:
- xbc: bfloat16 [16, 8192, 2688], P('bal', 'ctx'), may hold values from -6 to 6
- dt_raw: bfloat16 [16, 8192, 40], P('bal', 'ctx'), may hold values from -4 to 4
- conv_weight: float32 [4, 2688], replicated, may hold values from -3 to 3
- conv_bias: float32 [2688], replicated, may hold values from -0.5 to 0.5
- dt_bias: float32 [40], replicated, may hold values from -3 to 0
- a_log: float32 [40], replicated, may hold values from -9.2 to -2.3
- d_skip: float32 [40], replicated, may hold values from 0.5 to 1.5
- grad_out: bfloat16 [16, 8192, 2560], P('bal', 'ctx'), may hold values from -6 to 6
- doc_lengths: int32 [16, 8], P('bal'), may hold values from 1 to 4096, 8192 in all within a row
Outputs:
- grad_xbc: bfloat16 [16, 8192, 2688], P('bal', 'ctx')
- grad_dt_raw: bfloat16 [16, 8192, 40], P('bal', 'ctx')
- grad_conv_weight: float32 [4, 2688], replicated
- grad_conv_bias: float32 [2688], replicated
- grad_dt_bias: float32 [40], replicated
- grad_a_log: float32 [40], replicated
- grad_d_skip: float32 [40], replicated
Inputs may be any that keep to these rules, and one draw needn't show every extreme that they name: `doc_lengths`: each row sums to 8192; its largest entry is exactly 4096.
All inputs are finite; a program needn't handle non-finite values.
Results may differ from a plain program's by a relative error of at most 0.013.
Values may be sent and summed in bfloat16 or wider, within the bound.
A program may use at most 128 MiB of HBM per device.

v0:
```python
import jax
import jax.numpy as jnp
import numpy as np
from jax import lax
from jax.experimental import pallas as pl
from jax.experimental.pallas import tpu as pltpu
from jax.sharding import PartitionSpec as P

H = 40
P_SIZE = 64
N = 64
DIN = H * P_SIZE
PAIRS = H // 2
HIGHEST = lax.Precision.HIGHEST
F32 = jnp.float32
BF16 = jnp.bfloat16


def from_behind(value, axis, steps):
    count = lax.axis_size(axis)
    leading, last = (max(0, -steps), min(count, count - steps))
    return lax.ppermute(value, axis, [(source, source + steps) for source in range(leading, last)])


def doc_index(lengths, positions):
    starts = jnp.cumsum(lengths) - lengths
    hits = (positions[:, None] >= starts[None, :]).astype(jnp.int32)
    return jnp.sum(hits, axis=1) - 1


def dot(a, b, ca, cb, precision=None):
    return lax.dot_general(
        a, b, (((ca,), (cb,)), ((), ())), precision=precision, preferred_element_type=F32
    )


def core_kernel(
    x_ref, dy_ref, bc_ref, cumc_ref, cumr_ref, stepc_ref, docc_ref, docr_ref, skip_ref,
    dx_ref, xdx_ref, col_ref, xdy_ref, dbc_ref,
    scores, masked, gacc,
):
    j = pl.program_id(0)
    length = x_ref.shape[0]

    @pl.when(j == 0)
    def _():
        b, c = bc_ref[:, :N], bc_ref[:, N:]
        scores[...] = dot(b, c, 1, 1)
        s = lax.broadcasted_iota(jnp.int32, (length, length), 0)
        t = lax.broadcasted_iota(jnp.int32, (length, length), 1)
        same = (docc_ref[...] == docr_ref[...]) & (t >= s)
        masked[...] = jnp.where(same, 0.0, -1e30)
        gacc[...] = jnp.zeros_like(gacc)

    x, dy = x_ref[...], dy_ref[...]
    lane = lax.broadcasted_iota(jnp.int32, (length, 2 * P_SIZE), 1)
    mixes = []
    total = None
    for h in range(2):
        xh = jnp.where((lane < P_SIZE) == (h == 0), x, jnp.zeros_like(x))
        dw = dot(xh, dy, 1, 1)
        gap = cumr_ref[0, h : h + 1, :] - cumc_ref[0, :, h : h + 1]
        ds = jnp.exp(jnp.minimum(gap, 0.0) + masked[...]) * stepc_ref[0, :, h : h + 1]
        w = ds * scores[...]
        part = dw * ds
        total = part if total is None else total + part
        col_ref[0, h : h + 1, :] = jnp.sum(dw * w, axis=0, keepdims=True)
        mixes.append(dot(w.astype(BF16), dy, 1, 0))
    gacc[...] += total
    mix = jnp.where(lane < P_SIZE, mixes[0], mixes[1])
    xf, dyf = x.astype(F32), dy.astype(F32)
    xm = xf * mix
    first = jnp.sum(jnp.where(lane < P_SIZE, xm, 0.0), axis=1, keepdims=True)
    second = jnp.sum(jnp.where(lane < P_SIZE, 0.0, xm), axis=1, keepdims=True)
    xdx_ref[0] = jnp.concatenate([first, second], axis=1)
    xdy_ref[0] = jnp.sum(xf * dyf, axis=0, keepdims=True)
    dx_ref[...] = (mix + skip_ref[0] * dyf).astype(BF16)

    @pl.when(j == PAIRS - 1)
    def _():
        b, c = bc_ref[:, :N], bc_ref[:, N:]
        g = gacc[...].astype(BF16)
        dbc_ref[:, :N] = dot(g, c, 1, 0)
        dbc_ref[:, N:] = dot(g, b, 0, 0)


def core(activated, dy, cum, step, docs, skip_wide):
    length = activated.shape[0]
    pair_col = lambda v: v.reshape(length, PAIRS, 2).transpose(1, 0, 2)
    cumr = cum.T.reshape(PAIRS, 2, length)
    wide = pl.BlockSpec((length, 2 * P_SIZE), lambda j: (0, j))
    colspec = pl.BlockSpec((1, length, 2), lambda j: (j, 0, 0))
    rowspec = pl.BlockSpec((1, 2, length), lambda j: (j, 0, 0))
    lanes = pl.BlockSpec((1, 1, 2 * P_SIZE), lambda j: (j, 0, 0))
    dx, xdx, col, xdy, dbc = pl.pallas_call(
        core_kernel,
        grid=(PAIRS,),
        in_specs=[
            wide,
            wide,
            pl.BlockSpec((length, 2 * N), lambda j: (0, PAIRS)),
            colspec,
            rowspec,
            colspec,
            pl.BlockSpec((length, 1), lambda j: (0, 0)),
            pl.BlockSpec((1, length), lambda j: (0, 0)),
            lanes,
        ],
        out_specs=[
            wide,
            colspec,
            rowspec,
            lanes,
            pl.BlockSpec((length, 2 * N), lambda j: (0, 0)),
        ],
        out_shape=[
            jax.ShapeDtypeStruct((length, DIN), BF16),
            jax.ShapeDtypeStruct((PAIRS, length, 2), F32),
            jax.ShapeDtypeStruct((PAIRS, 2, length), F32),
            jax.ShapeDtypeStruct((PAIRS, 1, 2 * P_SIZE), F32),
            jax.ShapeDtypeStruct((length, 2 * N), F32),
        ],
        scratch_shapes=[pltpu.VMEM((length, length), F32)] * 3,
        cost_estimate=pl.CostEstimate(
            flops=4 * H * length * length * 2 * P_SIZE,
            bytes_accessed=8 * length * DIN,
            transcendentals=H * length * length,
        ),
        name="core",
    )(
        activated, dy, activated, pair_col(cum), cumr, pair_col(step),
        docs[:, None], docs[None, :], skip_wide.reshape(PAIRS, 1, 2 * P_SIZE),
    )
    back = lambda v: v.transpose(1, 0, 2).reshape(length, H)
    return dx, back(xdx), col.reshape(H, length).T, xdy, dbc


def scan_kernel(parts_ref, decay_ref, out_ref):
    count = parts_ref.shape[0]
    zero = jnp.zeros(parts_ref.shape[1:], F32)
    rows = parts_ref.shape[1] // 2
    forward = zero[:rows]
    for b in range(count):
        out_ref[b, :rows] = forward.astype(BF16)
        forward = decay_ref[b : b + 1] * forward + parts_ref[b, :rows].astype(F32)
    backward = zero[:rows]
    for b in reversed(range(count)):
        out_ref[b, rows:] = backward.astype(BF16)
        backward = decay_ref[b : b + 1] * backward + parts_ref[b, rows:].astype(F32)


def per_device(xbc, dt_raw, conv_weight, conv_bias, dt_bias, a_log, d_skip, grad_out, doc_lengths):
    taps = conv_weight.shape[0]
    own_rows = xbc[0]
    length = own_rows.shape[0]
    count = lax.axis_size("ctx")
    dy = grad_out[0]
    expand = jnp.asarray(np.kron(np.eye(H), np.ones((1, P_SIZE))), F32)
    widen = lambda v: dot(v, expand, 1, 0, HIGHEST)
    narrow = lambda v: dot(v, expand, 1, 1, HIGHEST)
    upto = jnp.tril(jnp.ones((length, length), F32))

    offset = lax.axis_index("ctx") * length
    positions = offset + jnp.arange(length + taps - 1, dtype=jnp.int32) - (taps - 1)
    docs_ext = doc_index(doc_lengths[0], positions)
    docs = docs_ext[taps - 1 :]
    prev_doc = docs_ext[taps - 2]
    rim_rows = from_behind(own_rows[length - taps + 1 :], "ctx", 1)
    extended = jnp.concatenate([rim_rows, own_rows], axis=0)
    keeps = [(docs_ext[k : k + length] == docs)[:, None] for k in range(taps)]
    shifted = [
        jnp.where(keeps[k], extended[k : k + length].astype(F32), 0.0) for k in range(taps)
    ]
    pre = conv_bias[None, :]
    for k in range(taps):
        pre = pre + conv_weight[k][None, :] * shifted[k]
    activated = jax.nn.silu(pre).astype(BF16)
    x = activated[:, :DIN].astype(F32)
    b, c = activated[:, DIN : DIN + N], activated[:, DIN + N :]

    raw = dt_raw[0].astype(F32) + dt_bias[None, :]
    step = jax.nn.softplus(raw)
    rate = -jnp.exp(a_log)
    cum = dot(upto, step * rate[None, :], 1, 0, HIGHEST)
    same_last = (docs == docs[-1]).astype(F32)[:, None]
    tail = jnp.exp(cum[-1][None, :] - cum) * same_last * step
    lead = jnp.exp(cum) * (docs == prev_doc).astype(F32)[:, None]
    decay = jnp.exp(cum[-1]) * (docs[-1] == prev_doc).astype(F32)
    tail_wide = widen(tail)
    weighted = (x * tail_wide).astype(BF16)
    led = (dy.astype(F32) * widen(lead)).astype(BF16)
    local = dot(b, weighted, 0, 0)
    seeded = dot(c, led, 0, 0)

    rows = N // count
    parts = jnp.concatenate(
        [local.reshape(count, rows, DIN), seeded.reshape(count, rows, DIN)], axis=1
    ).astype(BF16)
    parts = lax.all_to_all(parts, "ctx", 0, 0, tiled=True)
    decays = widen(lax.all_gather(decay, "ctx"))
    carried = pl.pallas_call(
        scan_kernel, out_shape=jax.ShapeDtypeStruct(parts.shape, BF16), name="carry"
    )(parts, decays)
    carried = lax.all_to_all(carried, "ctx", 0, 0, tiled=True)
    incoming = carried[:, :rows].reshape(N, DIN)
    adjoint = carried[:, rows:].reshape(N, DIN)

    dx, xdx, col, xdy, dbc = core(activated, dy, cum, step, docs, jnp.repeat(d_skip, P_SIZE))
    outer = dot(c, incoming, 1, 0)
    spread = dot(b, adjoint, 1, 0)
    from_lead = narrow(led.astype(F32) * outer)
    from_tail = narrow(spread * weighted.astype(F32))
    db = dbc[:, :N] + dot(weighted, adjoint, 1, 1)
    dc = dbc[:, N:] + dot(led, incoming, 1, 1)
    grad_act = jnp.concatenate([dx.astype(F32) + spread * tail_wide, db, dc], axis=1)
    grad_act = grad_act.astype(BF16).astype(F32)

    met = jnp.sum(adjoint.astype(F32) * incoming.astype(F32), axis=0, keepdims=True)
    grad_last = jnp.sum(from_tail, axis=0) + narrow(met)[0] * decay
    grad_cum = col - xdx + from_lead - from_tail
    grad_scaled = dot(upto, grad_cum, 0, 0, HIGHEST) + grad_last[None, :]
    grad_step = (xdx + from_tail) / step + grad_scaled * rate[None, :]
    grad_alog = jnp.sum(grad_scaled * step, axis=0) * rate
    grad_raw = grad_step * jax.nn.sigmoid(raw)
    grad_raw16 = grad_raw.astype(BF16)
    grad_dtb = jnp.sum(grad_raw, axis=0)
    grad_skip = jnp.sum(xdy.reshape(H, P_SIZE), axis=1)

    gate = jax.nn.sigmoid(pre)
    grad_pre = grad_act * (gate * (1.0 + pre * (1.0 - gate)))
    grad_weight = jnp.stack([jnp.sum(grad_pre * shifted[k], axis=0) for k in range(taps)])
    grad_bias = jnp.sum(grad_pre, axis=0)
    grad_ext = 0.0
    for k in range(taps):
        term = jnp.where(keeps[k], conv_weight[k][None, :] * grad_pre, 0.0)
        grad_ext = grad_ext + jnp.pad(term, ((k, taps - 1 - k), (0, 0)))
    grad_ext = grad_ext.astype(BF16)
    returned = from_behind(grad_ext[: taps - 1], "ctx", -1).astype(F32)
    own_grad = grad_ext[taps - 1 :].astype(F32)
    own_grad = own_grad + jnp.pad(returned, ((length - taps + 1, 0), (0, 0)))
    sums = lax.psum((grad_weight, grad_bias, grad_dtb, grad_alog, grad_skip), ("ctx", "bal"))
    return (own_grad.astype(BF16)[None], grad_raw16[None], *sums)


def solution(mesh):
    in_specs = (
        P("bal", "ctx", None),
        P("bal", "ctx", None),
        P(),
        P(),
        P(),
        P(),
        P(),
        P("bal", "ctx", None),
        P("bal", None),
    )
    out_specs = (P("bal", "ctx", None), P("bal", "ctx", None), P(), P(), P(), P(), P())
    return jax.shard_map(
        per_device, mesh=mesh, in_specs=in_specs, out_specs=out_specs, check_vma=False
    )
```

profile of v0, /device:TPU:1, one launch (start us, length us, event | category | flops | bytes accessed | tf_op | source)
XLA Modules:
  0.0 293.0 jit_solution(4656960971108200271)
XLA Ops:
  1.4 4.9 %collective-permute-start = (bf16[3,2688]{1,0:T(4,128)(2,1)S(1)}, bf16[3,2688]{1,0:T(4,128)(2,1)S(1)}, u32[]{:S(2)}, u32[]{:S(2)}) collective-permute-start(bf16[3,2688]{1,0:T(4,128)(2,1)S(1)} %slice_bitcast_fusion), channel_id=1, source_target_pairs={{0,16},{16,32},{32,48},{48,64},{64,80},{80,96},{96,112},{112,128},... | collective-permute-start | bytes 48392 | tf_op jit(solution)/shard_map/ppermute | solution.py:22
  9.9 1.9 compare_convert_fusion.1
  14.7 3.8 %fusion = bf16[256,2560]{1,0:T(8,128)(2,1)S(1)} fusion(f32[40,2560]{1,0:T(8,128)} %constant.37.clone, f32[256,40]{0,1:T(8,128)S(1)} %fusion.13, f32[256]{0:T(256)S(1)} %get-tuple-element.53, bf16[1,256,2560]{2,1,0:T(8,128)(2,1)} %param.17), kind=kOutput, calls=%fused_computation.2 | convolution fusion | flops 316549120 | bytes 3073024 | tf_op jit(solution)/shard_map/dot_general | solution.py:32
  19.2 4.0 %multiply_convert_fusion = (bf16[256,2688]{1,0:T(8,128)(2,1)S(1)}, f32[256,2688]{1,0:T(8,128)}) fusion(bf16[256,2688]{1,0:T(8,128)(2,1)S(1)} %bitcast.73, f32[2688]{0:T(1024)S(1)} %get-tuple-element.27, bf16[3,2688]{1,0:T(4,128)(2,1)S(1)} %collective-permute-done, pred[256]{0:T(512)(128)(4,1)S(1)} %get-tuple-element.54, f32[2688]{0:T(1024)S(1)} %get-tuple-element.28, ...), kind=kLoop, calls=%fused_computation.18 | loop fusion | flops 19955712 | bytes 5575680 | tf_op jit(solution)/shard_map/convert_element_type | solution.py:177
  25.6 4.7 %multiply_convert_fusion.1 = (bf16[256,2560]{1,0:T(8,128)(2,1)S(1)}, f32[256,2560]{1,0:T(8,128)}) fusion(bf16[256,2688]{1,0:T(8,128)(2,1)S(1)} %get-tuple-element.41.x_ref.bc_ref, f32[40,2560]{1,0:T(8,128)S(1)} %copy-done.3, f32[256,40]{0,1:T(8,128)S(1)} %fusion.13, f32[256]{0:T(256)} %get-tuple-element.52, f32[40]{0:T(128)} %get-tuple-element.30, ...), kind=kOutput, calls=%fused_computation.27 | convolution fusion | flops 316651520 | bytes 5715264 | tf_op jit(solution)/shard_map/dot_general | solution.py:32
  35.1 14.6 %all-to-all-start = ((bf16[32,4,2560]{2,1,0:T(4,128)(2,1)}), bf16[32,4,2560]{2,1,0:T(4,128)(2,1)S(1)}, u32[]{:S(2)}, u32[]{:S(2)}) async-start(bf16[32,4,2560]{2,1,0:T(4,128)(2,1)} %pad_maximum_fusion.1), calls=%async_computation | async-start | bytes 1310720 | tf_op jit(solution)/shard_map/all_to_all | solution.py:199
  49.7 54.9 %all-gather = f32[32,1,40]{2,1,0:T(1,128)S(1)} all-gather(f32[1,1,40]{2,1,0:T(1,128)S(1)} %bitcast.83), channel_id=1, replica_groups=mesh['ctx'=32,'bal'=16] {'ctx'}, dimensions={0}, use_global_device_ids=true | all-gather | bytes 5280 | tf_op jit(solution)/shard_map/all_gather | solution.py:200
  106.6 3.0 %carry.1 = bf16[32,4,2560]{2,1,0:T(4,128)(2,1)} custom-call(bf16[32,4,2560]{2,1,0:T(4,128)(2,1)} %copy-done.10, f32[32,2560]{1,0:T(8,128)} %fusion.49.decay_ref), custom_call_target="tpu_custom_call" | custom-call | tf_op jit(solution)/shard_map/carry/pallas_call | solution.py:201
  109.5 10.4 %all-to-all-start.1 = ((bf16[32,4,2560]{2,1,0:T(4,128)(2,1)}), bf16[32,4,2560]{2,1,0:T(4,128)(2,1)S(1)}, u32[]{:S(2)}, u32[]{:S(2)}) async-start(bf16[32,4,2560]{2,1,0:T(4,128)(2,1)} %carry.1), calls=%async_computation.1 | async-start | bytes 1310720 | tf_op jit(solution)/shard_map/all_to_all | solution.py:204
  123.7 2.3 copy.45
  125.9 2.3 copy.49
  128.3 4.7 %select_bitcast_fusion.stepc_ref = f32[20,256,2]{2,1,0:T(8,128)} fusion(pred[256,20,2]{2,0,1:T(8,128)(4,1)S(1)} %copy.48, f32[256,20,2]{2,0,1:T(8,128)} %copy.49), kind=kLoop, calls=%fused_computation.28 | loop fusion | flops 51200 | bytes 92160 | tf_op jit(solution)/shard_map/transpose | solution.py:89
  133.0 18.1 %core.1 = (bf16[256,2560]{1,0:T(8,128)(2,1)}, f32[20,256,2]{2,1,0:T(8,128)}, f32[20,2,256]{2,1,0:T(2,128)}, f32[20,1,128]{2,1,0:T(1,128)}, f32[256,128]{1,0:T(8,128)}) custom-call(bf16[256,2688]{1,0:T(8,128)(2,1)} %copy-done, bf16[256,2560]{1,0:T(8,128)(2,1)} %bitcast.76, bf16[256,2688]{1,0:T(8,128)(2,1)} %copy-done, f32[20,256,2]{2,1,0:T(8,128)} %bitcast.75, ...), custom_call_target="tpu_custom_call" | custom-call | flops 1342177280 | bytes 5242880 | tf_op jit(solution)/shard_map/core/pallas_call | solution.py:95
  152.0 2.5 copy.53
  155.2 3.8 %all-to-all-done.1 = bf16[32,4,2560]{2,1,0:T(4,128)(2,1)S(1)} async-done(((bf16[32,4,2560]{2,1,0:T(4,128)(2,1)}), bf16[32,4,2560]{2,1,0:T(4,128)(2,1)S(1)}, u32[]{:S(2)}, u32[]{:S(2)}) %all-to-all-start.1) | async-done | bytes 655392 | tf_op jit(solution)/shard_map/all_to_all | solution.py:204
  160.1 2.9 convolution_multiply_fusion
  164.6 3.0 %fusion.48 = (f32[40]{0:T(128)}, f32[256,40]{0,1:T(8,128)S(1)}) fusion(f32[40,2560]{1,0:T(8,128)S(1)} %copy-done.3, f32[256,2560]{1,0:T(8,128)S(1)} %fusion.21, bf16[256,2560]{1,0:T(8,128)(2,1)S(1)} %copy-done.2), kind=kOutput, calls=%fused_computation.108 | convolution fusion | flops 315893728 | bytes 4382880 | tf_op jit(solution)/shard_map/dot_general | solution.py:32
  169.8 2.5 concatenate.13
  172.3 5.2 %fusion.42 = (f32[2688]{0:T(1024)S(1)}, f32[2688]{0:T(1024)S(1)}, f32[2688]{0:T(1024)S(1)}, f32[2688]{0:T(1024)S(1)}, f32[2688]{0:T(1024)S(1)}, /*index=5*/f32[256,2688]{1,0:T(8,128)S(1)}) fusion(bf16[1,256,2688]{2,1,0:T(8,128)(2,1)S(1)} %copy-done.5, bf16[256,2688]{1,0:T(8,128)(2,1)S(1)} %bitcast.74, bf16[3,2688]{1,0:T(4,128)(2,1)S(1)} %copy-done.14, ...), kind=kLoop, calls=%fused_computation.103 | loop fusion | flops 23382912 | bytes 9704448 | tf_op jit(solution)/shard_map/reduce_sum | solution.py:232
  178.7 2.0 add_convert_fusion
  181.5 2.4 collective-permute-start.1
  184.4 2.4 fusion.9
  187.9 102.3 %all-reduce.5 = (f32[4,2688]{1,0:T(4,128)}, f32[2688]{0:T(1024)}, f32[40]{0:T(128)}, f32[40]{0:T(128)}, f32[40]{0:T(128)}) all-reduce(f32[4,2688]{1,0:T(4,128)S(1)} %pad_maximum_fusion.2, f32[2688]{0:T(1024)S(1)} %get-tuple-element.20, f32[40]{0:T(128)S(1)} %get-tuple-element.36, ...), channel_id=1, replica_groups=mesh['ctx'=32,'bal'=16] {'ctx','bal'}, use_global_device_ids=true, to_apply=%region_8.9 | all-reduce | flops 13560 | bytes 108480 | tf_op jit(solution)/shard_map/psum | solution.py:241
  290.2 2.8 fusion.8
  (124 shorter events, 29.0 us)
Async XLA Ops:
  0.6 18.5 %copy-start.17 = (f32[2688]{0:T(1024)S(1)}, f32[2688]{0:T(1024)}, u32[]{:S(2)}) copy-start(f32[2688]{0:T(1024)} %param.13) | copy-start | bytes 32260
  1.4 17.7 %collective-permute-start = (bf16[3,2688]{1,0:T(4,128)(2,1)S(1)}, bf16[3,2688]{1,0:T(4,128)(2,1)S(1)}, u32[]{:S(2)}, u32[]{:S(2)}) collective-permute-start(bf16[3,2688]{1,0:T(4,128)(2,1)S(1)} %slice_bitcast_fusion), channel_id=1, source_target_pairs={{0,16},{16,32},{32,48},{48,64},{64,80},{80,96},{96,112},{112,128},... | collective-permute-start | bytes 48392 | tf_op jit(solution)/shard_map/ppermute | solution.py:22
  11.8 11.4 %copy-start.19 = (pred[256]{0:T(512)(128)(4,1)}, pred[256]{0:T(512)(128)(4,1)S(1)}, u32[]{:S(2)}) copy-start(pred[256]{0:T(512)(128)(4,1)S(1)} %get-tuple-element.54) | copy-start | bytes 772
  11.8 11.4 %copy-start.21 = (pred[256]{0:T(512)(128)(4,1)}, pred[256]{0:T(512)(128)(4,1)S(1)}, u32[]{:S(2)}) copy-start(pred[256]{0:T(512)(128)(4,1)S(1)} %get-tuple-element.55) | copy-start | bytes 772
  11.8 11.4 %copy-start.23 = (pred[256]{0:T(512)(128)(4,1)}, pred[256]{0:T(512)(128)(4,1)S(1)}, u32[]{:S(2)}) copy-start(pred[256]{0:T(512)(128)(4,1)S(1)} %get-tuple-element.56) | copy-start | bytes 772
  12.5 10.8 %copy-start.32 = (f32[40]{0:T(128)}, f32[40]{0:T(128)S(1)}, u32[]{:S(2)}) copy-start(f32[40]{0:T(128)S(1)} %exponential_negate_fusion) | copy-start | bytes 484
  12.5 6.7 %copy-start.4 = (bf16[1,256,2688]{2,1,0:T(8,128)(2,1)S(1)}, bf16[1,256,2688]{2,1,0:T(8,128)(2,1)}, u32[]{:S(2)}) copy-start(bf16[1,256,2688]{2,1,0:T(8,128)(2,1)} %param.10) | copy-start | bytes 4128772
  19.2 6.4 %copy-start.3 = (f32[40,2560]{1,0:T(8,128)S(1)}, f32[40,2560]{1,0:T(8,128)}, u32[]{:S(2)}) copy-start(f32[40,2560]{1,0:T(8,128)} %constant.37.clone) | copy-start | bytes 1228804
  23.2 7.0 %copy-start = (bf16[256,2688]{1,0:T(8,128)(2,1)}, bf16[256,2688]{1,0:T(8,128)(2,1)S(1)}, u32[]{:S(2)}) copy-start(bf16[256,2688]{1,0:T(8,128)(2,1)S(1)} %get-tuple-element.41.x_ref.bc_ref) | copy-start | bytes 4128772
  30.3 19.4 %copy-start.29 = (f32[40]{0:T(128)S(1)}, f32[40]{0:T(128)}, u32[]{:S(2)}) copy-start(f32[40]{0:T(128)} %get-tuple-element.29) | copy-start | bytes 484
  35.1 84.9 %copy-start.25 = (f32[40]{0:T(128)S(1)}, f32[40]{0:T(128)}, u32[]{:S(2)}) copy-start(f32[40]{0:T(128)} %param.14) | copy-start | bytes 484
  35.1 85.1 %copy-start.15 = (bf16[1,256,40]{1,2,0:T(8,128)(2,1)S(1)}, bf16[1,256,40]{1,2,0:T(8,128)(2,1)}, u32[]{:S(2)}) copy-start(bf16[1,256,40]{1,2,0:T(8,128)(2,1)} %param.11) | copy-start | bytes 61444
  35.1 85.1 %copy-start.30 = (f32[40]{0:T(128)S(1)}, f32[40]{0:T(128)}, u32[]{:S(2)}) copy-start(f32[40]{0:T(128)} %param.16) | copy-start | bytes 484
  35.1 70.6 %all-to-all-start = ((bf16[32,4,2560]{2,1,0:T(4,128)(2,1)}), bf16[32,4,2560]{2,1,0:T(4,128)(2,1)S(1)}, u32[]{:S(2)}, u32[]{:S(2)}) async-start(bf16[32,4,2560]{2,1,0:T(4,128)(2,1)} %pad_maximum_fusion.1), calls=%async_computation | async-start | bytes 1310720 | tf_op jit(solution)/shard_map/all_to_all | solution.py:199
  109.5 49.5 %all-to-all-start.1 = ((bf16[32,4,2560]{2,1,0:T(4,128)(2,1)}), bf16[32,4,2560]{2,1,0:T(4,128)(2,1)S(1)}, u32[]{:S(2)}, u32[]{:S(2)}) async-start(bf16[32,4,2560]{2,1,0:T(4,128)(2,1)} %carry.1), calls=%async_computation.1 | async-start | bytes 1310720 | tf_op jit(solution)/shard_map/all_to_all | solution.py:204
  120.0 8.2 %copy-start.18 = (s32[256]{0:T(256)}, s32[256]{0:T(256)S(1)}, u32[]{:S(2)}) copy-start(s32[256]{0:T(256)S(1)} %slice.84) | copy-start | bytes 3076
  172.3 5.3 %copy-start.22 = (pred[256]{0:T(512)(128)(4,1)S(1)}, pred[256]{0:T(512)(128)(4,1)}, u32[]{:S(2)}) copy-start(pred[256]{0:T(512)(128)(4,1)} %copy-done.21) | copy-start | bytes 772
  172.3 5.3 %copy-start.24 = (pred[256]{0:T(512)(128)(4,1)S(1)}, pred[256]{0:T(512)(128)(4,1)}, u32[]{:S(2)}) copy-start(pred[256]{0:T(512)(128)(4,1)} %copy-done.23) | copy-start | bytes 772
  178.7 5.7 %copy-start.6 = (f32[256,2560]{1,0:T(8,128)S(1)}, f32[256,2560]{1,0:T(8,128)}, u32[]{:S(2)}) copy-start(f32[256,2560]{1,0:T(8,128)} %convolution_multiply_fusion) | copy-start | bytes 7864324
  180.7 6.1 %copy-start.26 = (f32[40]{0:T(128)S(1)}, f32[40]{0:T(128)}, u32[]{:S(2)}) copy-start(f32[40]{0:T(128)} %param.14) | copy-start | bytes 484
  180.7 6.1 %copy-start.33 = (f32[40]{0:T(128)S(1)}, f32[40]{0:T(128)}, u32[]{:S(2)}) copy-start(f32[40]{0:T(128)} %copy-done.32) | copy-start | bytes 484
  180.7 7.2 %copy-start.31 = (f32[40]{0:T(128)S(1)}, f32[40]{0:T(128)}, u32[]{:S(2)}) copy-start(f32[40]{0:T(128)} %param.15) | copy-start | bytes 484
  180.7 7.2 %copy-start.27 = (f32[40]{0:T(128)S(1)}, f32[40]{0:T(128)}, u32[]{:S(2)}) copy-start(f32[40]{0:T(128)} %reduce_sum.112) | copy-start | bytes 484
  181.5 108.8 %collective-permute-start.1 = (bf16[3,2688]{1,0:T(4,128)(2,1)S(1)}, bf16[3,2688]{1,0:T(4,128)(2,1)S(1)}, u32[]{:S(2)}, u32[]{:S(2)}) collective-permute-start(bf16[3,2688]{1,0:T(4,128)(2,1)S(1)} %add_convert_fusion.5), channel_id=1, source_target_pairs={{16,0},{32,16},{48,32},{64,48},{80,64},{96,80},{112,96},{128,112},... | collective-permute-start | bytes 48392 | tf_op jit(solution)/shard_map/ppermute | solution.py:22
  (14 other events, 37.3 us)
where the time goes:
time: 295 us; the launch traced here: 293 us
  blocking collectives  157 us (53%)
  starting transfers between devices  32.3 us (11%)
  other arithmetic  29.9 us (10%)
  matrix products  25.2 us (9%)
  Pallas kernels  21.1 us (7%)
  local copies, waits for them, and re-layouts  20.9 us (7%)
  waiting for transfers between devices  3.85 us (1%)
    psum x1, blocking collectives, per_device(): lax.psum((grad_weight, grad_bias, grad_dtb, grad_alog, grad_skip), ('ctx'...  102 us
    all_gather x1, blocking collectives, per_device(): decays = widen(lax.all_gather(decay, 'ctx'))  54.9 us
    dot_general x13, matrix products, dot(): lax.dot_general(a, b, (((ca,), (cb,)), ((), ())), precision=precision, pr...  24.7 us
    pallas_call x1, Pallas kernels, core(): pl.pallas_call(core_kernel, grid=(PAIRS,), in_specs=[wide, wide, pl.Block...  18.1 us
    all_to_all x1, starting transfers between devices, per_device(): parts = lax.all_to_all(parts, 'ctx', 0, 0, tiled=True)  14.6 us
    all_to_all x1, starting transfers between devices, per_device(): carried = lax.all_to_all(carried, 'ctx', 0, 0, tiled=True)  10.4 us
    ppermute x2, starting transfers between devices, from_behind(): lax.ppermute(value, axis, [(source, source + steps) for source in range(l...  7.32 us
  transfers between devices with their start and end apart: 4, of which 1 were waited for; matrix products, arithmetic and copies ran while one was open for 11% of the time, Pallas kernels for 6%

commit v1 on v0

--- a/solution.py
+++ b/solution.py
@@ -35,8 +35,8 @@
 
 
 def core_kernel(
-    x_ref, dy_ref, bc_ref, cumc_ref, cumr_ref, stepc_ref, docc_ref, docr_ref, skip_ref,
-    dx_ref, xdx_ref, col_ref, xdy_ref, dbc_ref,
+    x_ref, dy_ref, bc_ref, steps_ref, docc_ref, docr_ref, skip_ref,
+    dx_ref, rows_ref, xdy_ref, dbc_ref,
     scores, masked, gacc,
 ):
     j = pl.program_id(0)
@@ -54,25 +54,30 @@
 
     x, dy = x_ref[...], dy_ref[...]
     lane = lax.broadcasted_iota(jnp.int32, (length, 2 * P_SIZE), 1)
+    rows = steps_ref[0]
+    cols = rows.T
     mixes = []
     total = None
     for h in range(2):
         xh = jnp.where((lane < P_SIZE) == (h == 0), x, jnp.zeros_like(x))
         dw = dot(xh, dy, 1, 1)
-        gap = cumr_ref[0, h : h + 1, :] - cumc_ref[0, :, h : h + 1]
-        ds = jnp.exp(jnp.minimum(gap, 0.0) + masked[...]) * stepc_ref[0, :, h : h + 1]
+        gap = rows[h : h + 1, :] - cols[:, h : h + 1]
+        ds = jnp.exp(jnp.minimum(gap, 0.0) + masked[...]) * cols[:, h + 2 : h + 3]
         w = ds * scores[...]
         part = dw * ds
         total = part if total is None else total + part
-        col_ref[0, h : h + 1, :] = jnp.sum(dw * w, axis=0, keepdims=True)
+        rows_ref[0, h + 2 : h + 3, :] = jnp.sum(dw * w, axis=0, keepdims=True)
         mixes.append(dot(w.astype(BF16), dy, 1, 0))
     gacc[...] += total
     mix = jnp.where(lane < P_SIZE, mixes[0], mixes[1])
     xf, dyf = x.astype(F32), dy.astype(F32)
     xm = xf * mix
-    first = jnp.sum(jnp.where(lane < P_SIZE, xm, 0.0), axis=1, keepdims=True)
-    second = jnp.sum(jnp.where(lane < P_SIZE, 0.0, xm), axis=1, keepdims=True)
-    xdx_ref[0] = jnp.concatenate([first, second], axis=1)
+    high = xm.astype(BF16)
+    low = (xm - high.astype(F32)).astype(BF16)
+    head = lax.broadcasted_iota(jnp.int32, (8, 2 * P_SIZE), 0)
+    pick = lax.broadcasted_iota(jnp.int32, (8, 2 * P_SIZE), 1) // P_SIZE == head
+    pick = jnp.where(pick, 1.0, 0.0).astype(BF16)
+    rows_ref[0, :2, :] = (dot(pick, high, 1, 1) + dot(pick, low, 1, 1))[:2]
     xdy_ref[0] = jnp.sum(xf * dyf, axis=0, keepdims=True)
     dx_ref[...] = (mix + skip_ref[0] * dyf).astype(BF16)
 
@@ -86,37 +91,33 @@
 
 def core(activated, dy, cum, step, docs, skip_wide):
     length = activated.shape[0]
-    pair_col = lambda v: v.reshape(length, PAIRS, 2).transpose(1, 0, 2)
-    cumr = cum.T.reshape(PAIRS, 2, length)
+    pairs = lambda v: v.reshape(PAIRS, 2, length)
+    packed = jnp.concatenate(
+        [pairs(cum), pairs(step), jnp.zeros((PAIRS, 4, length), F32)], axis=1
+    )
     wide = pl.BlockSpec((length, 2 * P_SIZE), lambda j: (0, j))
-    colspec = pl.BlockSpec((1, length, 2), lambda j: (j, 0, 0))
-    rowspec = pl.BlockSpec((1, 2, length), lambda j: (j, 0, 0))
     lanes = pl.BlockSpec((1, 1, 2 * P_SIZE), lambda j: (j, 0, 0))
-    dx, xdx, col, xdy, dbc = pl.pallas_call(
+    dx, rows, xdy, dbc = pl.pallas_call(
         core_kernel,
         grid=(PAIRS,),
         in_specs=[
             wide,
             wide,
             pl.BlockSpec((length, 2 * N), lambda j: (0, PAIRS)),
-            colspec,
-            rowspec,
-            colspec,
+            pl.BlockSpec((1, 8, length), lambda j: (j, 0, 0)),
             pl.BlockSpec((length, 1), lambda j: (0, 0)),
             pl.BlockSpec((1, length), lambda j: (0, 0)),
             lanes,
         ],
         out_specs=[
             wide,
-            colspec,
-            rowspec,
+            pl.BlockSpec((1, 4, length), lambda j: (j, 0, 0)),
             lanes,
             pl.BlockSpec((length, 2 * N), lambda j: (0, 0)),
         ],
         out_shape=[
             jax.ShapeDtypeStruct((length, DIN), BF16),
-            jax.ShapeDtypeStruct((PAIRS, length, 2), F32),
-            jax.ShapeDtypeStruct((PAIRS, 2, length), F32),
+            jax.ShapeDtypeStruct((PAIRS, 4, length), F32),
             jax.ShapeDtypeStruct((PAIRS, 1, 2 * P_SIZE), F32),
             jax.ShapeDtypeStruct((length, 2 * N), F32),
         ],
@@ -128,25 +129,215 @@
         ),
         name="core",
     )(
-        activated, dy, activated, pair_col(cum), cumr, pair_col(step),
+        activated, dy, activated, packed,
         docs[:, None], docs[None, :], skip_wide.reshape(PAIRS, 1, 2 * P_SIZE),
     )
-    back = lambda v: v.transpose(1, 0, 2).reshape(length, H)
-    return dx, back(xdx), col.reshape(H, length).T, xdy, dbc
-
-
-def scan_kernel(parts_ref, decay_ref, out_ref):
-    count = parts_ref.shape[0]
-    zero = jnp.zeros(parts_ref.shape[1:], F32)
+    xdx, col = rows[:, :2].reshape(H, length), rows[:, 2:].reshape(H, length)
+    return dx, xdx, col, xdy, dbc
+
+
+def total_kernel(
+    v_ref, out_ref, got, mid, across, last, spread,
+    send_a, recv_a, send_b, recv_b, send_c, recv_c,
+):
+    nc, nb = lax.axis_size("ctx"), lax.axis_size("bal")
+    ctx, bal = lax.axis_index("ctx"), lax.axis_index("bal")
+
+    def to_ctx(k):
+        return lax.rem(ctx + k, nc)
+
+    def to_bal(k):
+        return lax.rem(bal + k, nb)
+
+    def send(src, dst, sends, recvs, axis, peer, k):
+        return pltpu.make_async_remote_copy(
+            src_ref=src, dst_ref=dst, send_sem=sends.at[k], recv_sem=recvs.at[k],
+            device_id={axis: peer}, device_id_type=pl.DeviceIdType.MESH,
+        )
+
+    barrier = pltpu.get_barrier_semaphore()
+
+    @pl.loop(1, nc)
+    def _(k):
+        pl.semaphore_signal(
+            barrier, 1, device_id={"ctx": to_ctx(k)}, device_id_type=pl.DeviceIdType.MESH
+        )
+
+    @pl.loop(1, nb)
+    def _(k):
+        pl.semaphore_signal(
+            barrier, 1, device_id={"bal": to_bal(k)}, device_id_type=pl.DeviceIdType.MESH
+        )
+
+    pl.semaphore_wait(barrier, nc + nb - 2)
+
+    def first(k):
+        return send(v_ref.at[to_ctx(k)], got.at[k], send_a, recv_a, "ctx", to_ctx(k), k)
+
+    def second(k):
+        return send(mid, across.at[bal], send_b, recv_b, "bal", to_bal(k), k)
+
+    def third(k):
+        return send(last, spread.at[ctx], send_c, recv_c, "ctx", to_ctx(k), k)
+
+    @pl.loop(1, nc)
+    def _(k):
+        first(k).start()
+
+    got[0] = v_ref[ctx]
+
+    @pl.loop(1, nc)
+    def _(k):
+        first(k).wait()
+
+    summed = jnp.sum(got[...], axis=0)
+    mid[...] = summed
+    across[bal] = summed
+
+    @pl.loop(1, nb)
+    def _(k):
+        second(k).start()
+
+    @pl.loop(1, nb)
+    def _(k):
+        second(k).wait()
+
+    summed = jnp.sum(across[...], axis=0)
+    last[...] = summed
+    spread[ctx] = summed
+
+    @pl.loop(1, nc)
+    def _(k):
+        third(k).start()
+
+    @pl.loop(1, nc)
+    def _(k):
+        third(k).wait()
+
+    out_ref[...] = spread[...]
+
+
+def total_sum(vector):
+    nc, nb = lax.axis_size("ctx"), lax.axis_size("bal")
+    rows = -(-vector.shape[0] // (nc * 128))
+    padded = jnp.pad(vector, (0, nc * rows * 128 - vector.shape[0])).reshape(nc, rows, 128)
+    dma = pltpu.SemaphoreType.DMA
+    summed = pl.pallas_call(
+        total_kernel,
+        out_shape=jax.ShapeDtypeStruct(padded.shape, F32),
+        in_specs=[pl.BlockSpec(memory_space=pltpu.VMEM)],
+        out_specs=pl.BlockSpec(memory_space=pltpu.VMEM),
+        scratch_shapes=[
+            pltpu.VMEM((nc, rows, 128), F32),
+            pltpu.VMEM((rows, 128), F32),
+            pltpu.VMEM((nb, rows, 128), F32),
+            pltpu.VMEM((rows, 128), F32),
+            pltpu.VMEM((nc, rows, 128), F32),
+            dma((nc,)), dma((nc,)), dma((nb,)), dma((nb,)), dma((nc,)), dma((nc,)),
+        ],
+        compiler_params=pltpu.CompilerParams(collective_id=0, has_side_effects=True),
+        name="total",
+    )(padded)
+    return summed.reshape(-1)[: vector.shape[0]]
+
+
+def exchange_kernel(
+    parts_ref, decay_ref, out_ref, got, decays, turned, result,
+    send_a, recv_a, send_d, recv_d, send_b, recv_b,
+):
+    nc = lax.axis_size("ctx")
+    ctx = lax.axis_index("ctx")
     rows = parts_ref.shape[1] // 2
-    forward = zero[:rows]
-    for b in range(count):
-        out_ref[b, :rows] = forward.astype(BF16)
-        forward = decay_ref[b : b + 1] * forward + parts_ref[b, :rows].astype(F32)
-    backward = zero[:rows]
-    for b in reversed(range(count)):
-        out_ref[b, rows:] = backward.astype(BF16)
-        backward = decay_ref[b : b + 1] * backward + parts_ref[b, rows:].astype(F32)
+
+    def peer(k):
+        return lax.rem(ctx + k, nc)
+
+    def send(src, dst, sends, recvs, k):
+        return pltpu.make_async_remote_copy(
+            src_ref=src, dst_ref=dst, send_sem=sends.at[k], recv_sem=recvs.at[k],
+            device_id={"ctx": peer(k)}, device_id_type=pl.DeviceIdType.MESH,
+        )
+
+    def both_ways(i):
+        half = (i + 1) // 2
+        return jnp.where(lax.rem(i, 2) == 1, half, nc - half)
+
+    barrier = pltpu.get_barrier_semaphore()
+
+    @pl.loop(1, nc)
+    def _(k):
+        pl.semaphore_signal(
+            barrier, 1, device_id={"ctx": peer(k)}, device_id_type=pl.DeviceIdType.MESH
+        )
+
+    pl.semaphore_wait(barrier, nc - 1)
+
+    def small(k):
+        return send(decay_ref, decays.at[ctx], send_d, recv_d, k)
+
+    def out(k):
+        return send(parts_ref.at[peer(k)], got.at[ctx], send_a, recv_a, k)
+
+    def back(k):
+        return send(turned.at[peer(k)], result.at[ctx], send_b, recv_b, k)
+
+    @pl.loop(1, nc)
+    def _(i):
+        small(both_ways(i)).start()
+        out(both_ways(i)).start()
+
+    decays[ctx] = decay_ref[...]
+    got[ctx] = parts_ref[ctx]
+
+    @pl.loop(1, nc)
+    def _(k):
+        small(k).wait()
+        out(k).wait()
+
+    shape = (128, parts_ref.shape[2])
+    head = lax.broadcasted_iota(jnp.int32, shape, 1) // P_SIZE
+    own = head == lax.broadcasted_iota(jnp.int32, shape, 0)
+    decay = dot(decays[:, 0, :], jnp.where(own, 1.0, 0.0), 1, 0, HIGHEST)
+    forward = jnp.zeros((rows, parts_ref.shape[2]), F32)
+    for b in range(nc):
+        turned[b, :rows] = forward.astype(BF16)
+        forward = decay[b : b + 1] * forward + got[b, :rows].astype(F32)
+    backward = jnp.zeros((rows, parts_ref.shape[2]), F32)
+    for b in reversed(range(nc)):
+        turned[b, rows:] = backward.astype(BF16)
+        backward = decay[b : b + 1] * backward + got[b, rows:].astype(F32)
+
+    @pl.loop(1, nc)
+    def _(i):
+        back(both_ways(i)).start()
+
+    result[ctx] = turned[ctx]
+
+    @pl.loop(1, nc)
+    def _(k):
+        back(k).wait()
+
+    out_ref[...] = result[...]
+
+
+def exchange(parts, decay):
+    nc = parts.shape[0]
+    dma = pltpu.SemaphoreType.DMA
+    return pl.pallas_call(
+        exchange_kernel,
+        out_shape=jax.ShapeDtypeStruct(parts.shape, BF16),
+        in_specs=[pl.BlockSpec(memory_space=pltpu.VMEM)] * 2,
+        out_specs=pl.BlockSpec(memory_space=pltpu.VMEM),
+        scratch_shapes=[
+            pltpu.VMEM(parts.shape, BF16),
+            pltpu.VMEM((nc, 1, 128), F32),
+            pltpu.VMEM(parts.shape, BF16),
+            pltpu.VMEM(parts.shape, BF16),
+            *[dma((nc,))] * 6,
+        ],
+        compiler_params=pltpu.CompilerParams(collective_id=1, has_side_effects=True),
+        name="exchange",
+    )(parts, jnp.pad(decay, (0, 128 - H))[None, :])
 
 
 def per_device(xbc, dt_raw, conv_weight, conv_bias, dt_bias, a_log, d_skip, grad_out, doc_lengths):
@@ -156,9 +347,9 @@
     count = lax.axis_size("ctx")
     dy = grad_out[0]
     expand = jnp.asarray(np.kron(np.eye(H), np.ones((1, P_SIZE))), F32)
-    widen = lambda v: dot(v, expand, 1, 0, HIGHEST)
-    narrow = lambda v: dot(v, expand, 1, 1, HIGHEST)
-    upto = jnp.tril(jnp.ones((length, length), F32))
+    widen = lambda v: dot(v, expand, 0, 0, HIGHEST)
+    narrow = lambda v: dot(expand, v, 1, 1, HIGHEST)
+    upto = jnp.triu(jnp.ones((length, length), F32))
 
     offset = lax.axis_index("ctx") * length
     positions = offset + jnp.arange(length + taps - 1, dtype=jnp.int32) - (taps - 1)
@@ -178,14 +369,14 @@
     x = activated[:, :DIN].astype(F32)
     b, c = activated[:, DIN : DIN + N], activated[:, DIN + N :]
 
-    raw = dt_raw[0].astype(F32) + dt_bias[None, :]
+    raw = dt_raw[0].T.astype(F32) + dt_bias[:, None]
     step = jax.nn.softplus(raw)
-    rate = -jnp.exp(a_log)
-    cum = dot(upto, step * rate[None, :], 1, 0, HIGHEST)
-    same_last = (docs == docs[-1]).astype(F32)[:, None]
-    tail = jnp.exp(cum[-1][None, :] - cum) * same_last * step
-    lead = jnp.exp(cum) * (docs == prev_doc).astype(F32)[:, None]
-    decay = jnp.exp(cum[-1]) * (docs[-1] == prev_doc).astype(F32)
+    rate = -jnp.exp(a_log)[:, None]
+    cum = dot(step * rate, upto, 1, 0, HIGHEST)
+    same_last = (docs == docs[-1]).astype(F32)[None, :]
+    tail = jnp.exp(cum[:, -1:] - cum) * same_last * step
+    lead = jnp.exp(cum) * (docs == prev_doc).astype(F32)[None, :]
+    decay = jnp.exp(cum[:, -1]) * (docs[-1] == prev_doc).astype(F32)
     tail_wide = widen(tail)
     weighted = (x * tail_wide).astype(BF16)
     led = (dy.astype(F32) * widen(lead)).astype(BF16)
@@ -196,12 +387,7 @@
     parts = jnp.concatenate(
         [local.reshape(count, rows, DIN), seeded.reshape(count, rows, DIN)], axis=1
     ).astype(BF16)
-    parts = lax.all_to_all(parts, "ctx", 0, 0, tiled=True)
-    decays = widen(lax.all_gather(decay, "ctx"))
-    carried = pl.pallas_call(
-        scan_kernel, out_shape=jax.ShapeDtypeStruct(parts.shape, BF16), name="carry"
-    )(parts, decays)
-    carried = lax.all_to_all(carried, "ctx", 0, 0, tiled=True)
+    carried = exchange(parts, decay)
     incoming = carried[:, :rows].reshape(N, DIN)
     adjoint = carried[:, rows:].reshape(N, DIN)
 
@@ -216,14 +402,14 @@
     grad_act = grad_act.astype(BF16).astype(F32)
 
     met = jnp.sum(adjoint.astype(F32) * incoming.astype(F32), axis=0, keepdims=True)
-    grad_last = jnp.sum(from_tail, axis=0) + narrow(met)[0] * decay
+    grad_last = jnp.sum(from_tail, axis=1, keepdims=True) + narrow(met) * decay[:, None]
     grad_cum = col - xdx + from_lead - from_tail
-    grad_scaled = dot(upto, grad_cum, 0, 0, HIGHEST) + grad_last[None, :]
-    grad_step = (xdx + from_tail) / step + grad_scaled * rate[None, :]
-    grad_alog = jnp.sum(grad_scaled * step, axis=0) * rate
+    grad_scaled = dot(grad_cum, upto, 1, 1, HIGHEST) + grad_last
+    grad_step = (xdx + from_tail) / step + grad_scaled * rate
+    grad_alog = jnp.sum(grad_scaled * step, axis=1) * rate[:, 0]
     grad_raw = grad_step * jax.nn.sigmoid(raw)
-    grad_raw16 = grad_raw.astype(BF16)
-    grad_dtb = jnp.sum(grad_raw, axis=0)
+    grad_raw16 = grad_raw.astype(BF16).T
+    grad_dtb = jnp.sum(grad_raw, axis=1)
     grad_skip = jnp.sum(xdy.reshape(H, P_SIZE), axis=1)
 
     gate = jax.nn.sigmoid(pre)
@@ -238,7 +424,10 @@
     returned = from_behind(grad_ext[: taps - 1], "ctx", -1).astype(F32)
     own_grad = grad_ext[taps - 1 :].astype(F32)
     own_grad = own_grad + jnp.pad(returned, ((length - taps + 1, 0), (0, 0)))
-    sums = lax.psum((grad_weight, grad_bias, grad_dtb, grad_alog, grad_skip), ("ctx", "bal"))
+    mine = (grad_weight, grad_bias, grad_dtb, grad_alog, grad_skip)
+    total = total_sum(jnp.concatenate([part.reshape(-1) for part in mine]))
+    ends = np.cumsum([part.size for part in mine])[:-1].tolist()
+    sums = [part.reshape(like.shape) for part, like in zip(jnp.split(total, ends), mine)]
     return (own_grad.astype(BF16)[None], grad_raw16[None], *sums)
 
 

time: 295 us -> 221 us (0.75)
  blocking collectives: 157 us -> 0 us
  Pallas kernels: 21.1 us -> 135 us
  starting transfers between devices: 32.3 us -> 7.25 us
  waiting for transfers between devices: 3.85 us -> 0.01 us
  matrix products: 25.2 us -> 28.9 us
  local copies, waits for them, and re-layouts: 20.9 us -> 17.2 us
    pallas_call x1 -> x2, Pallas kernels: 2.99 us -> 117 us  [the longest x1 83.9 us: exchange(): pl.pallas_call(exchange_kernel, out_shape=jax.ShapeDtypeStruct(parts.shap...]
    psum x1 -> x0, blocking collectives: 102 us -> none  [per_device(): lax.psum((grad_weight, grad_bias, grad_dtb, grad_alog, grad_skip), ('ctx'...]
    all_gather x1 -> x0, blocking collectives: 54.9 us -> none  [per_device(): decays = widen(lax.all_gather(decay, 'ctx'))]
    all_to_all x2 -> x0, starting transfers between devices: 25 us -> none  [the longest x1 14.6 us: per_device(): parts = lax.all_to_all(parts, 'ctx', 0, 0, tiled=True)]
    transpose x1 -> x0, other arithmetic: 4.71 us -> none  [core(): pair_col = lambda v: v.reshape(length, PAIRS, 2).transpose(1, 0, 2)]
    dot_general x13, matrix products: 24.7 us -> 28.9 us  [dot(): lax.dot_general(a, b, (((ca,), (cb,)), ((), ())), precision=precision, pr...]
    all_to_all x2 -> x0, waiting for transfers between devices: 3.85 us -> none  [the longest x1 3.85 us: per_device(): carried = lax.all_to_all(carried, 'ctx', 0, 0, tiled=True)]
    split x0 -> x3, local copies, waits for them, and re-layouts: none -> 3.48 us  [per_device(): jnp.split(total, ends)]
  transfers between devices with their start and end apart: 4 -> 2, of which waited for: 1 -> 0; matrix products, arithmetic and copies ran while one was open for 11% -> 8% of each run, Pallas kernels for 6% -> 0%
where the time goes in v1:
time: 221 us; the launch traced here: 219 us
  Pallas kernels  135 us (61%)
  matrix products  28.9 us (13%)
  other arithmetic  28.3 us (13%)
  local copies, waits for them, and re-layouts  17.2 us (8%)
  starting transfers between devices  7.25 us (3%)
  between operations  2.69 us (1%)
    pallas_call x1, Pallas kernels, exchange(): pl.pallas_call(exchange_kernel, out_shape=jax.ShapeDtypeStruct(parts.shap...  83.9 us
    pallas_call x1, Pallas kernels, total_sum(): pl.pallas_call(total_kernel, out_shape=jax.ShapeDtypeStruct(padded.shape,...  33.2 us
    dot_general x13, matrix products, dot(): lax.dot_general(a, b, (((ca,), (cb,)), ((), ())), precision=precision, pr...  28.9 us
    pallas_call x1, Pallas kernels, core(): pl.pallas_call(core_kernel, grid=(PAIRS,), in_specs=[wide, wide, pl.Block...  17.8 us
    ppermute x2, starting transfers between devices, from_behind(): lax.ppermute(value, axis, [(source, source + steps) for source in range(l...  7.25 us
    reduce_sum x1, other arithmetic, per_device(): grad_bias = jnp.sum(grad_pre, axis=0)  5.13 us
  transfers between devices with their start and end apart: 2, of which 0 were waited for; matrix products, arithmetic and copies ran while one was open for 8% of the time, Pallas kernels for 0%

profile of v1, /device:TPU:1, one launch (start us, length us, event | category | flops | bytes accessed | tf_op | source)
XLA Modules:
  0.0 219.2 jit_solution(17928350568227154630)
XLA Ops:
  1.6 4.9 %collective-permute-start = (bf16[3,2688]{1,0:T(4,128)(2,1)S(1)}, bf16[3,2688]{1,0:T(4,128)(2,1)S(1)}, u32[]{:S(2)}, u32[]{:S(2)}) collective-permute-start(bf16[3,2688]{1,0:T(4,128)(2,1)S(1)} %slice_bitcast_fusion), channel_id=1, source_target_pairs={{0,16},{16,32},{32,48},{48,64},{64,80},{80,96},{96,112},{112,128},... | collective-permute-start | bytes 48392 | tf_op jit(solution)/shard_map/ppermute | solution.py:22
  10.0 1.4 compare_convert_fusion.1
  16.2 3.8 %fusion = bf16[256,2560]{1,0:T(8,128)(2,1)S(1)} fusion(f32[40,2560]{1,0:T(8,128)} %constant.40.clone, f32[40,256]{1,0:T(8,128)S(1)} %fusion.13, f32[256]{0:T(256)S(1)} %get-tuple-element.47, bf16[1,256,2560]{2,1,0:T(8,128)(2,1)} %param.17), kind=kOutput, calls=%fused_computation.2 | convolution fusion | flops 316549120 | bytes 3073024 | tf_op jit(solution)/shard_map/dot_general | solution.py:32
  22.3 4.4 %multiply_convert_fusion = (bf16[256,2688]{1,0:T(8,128)(2,1)}, f32[256,2688]{1,0:T(8,128)}) fusion(bf16[256,2688]{1,0:T(8,128)(2,1)S(1)} %bitcast.115, f32[2688]{0:T(1024)S(1)} %get-tuple-element.25, bf16[3,2688]{1,0:T(4,128)(2,1)S(1)} %collective-permute-done, pred[256]{0:T(512)(128)(4,1)S(1)} %get-tuple-element.48, f32[2688]{0:T(1024)S(1)} %get-tuple-element.26, ...), kind=kLoop, calls=%fused_computation.18 | loop fusion | flops 19955712 | bytes 5575680 | tf_op jit(solution)/shard_map/convert_element_type | solution.py:368
  28.2 5.2 %multiply_convert_fusion.1 = (bf16[256,2560]{1,0:T(8,128)(2,1)S(1)}, f32[256,2560]{1,0:T(8,128)}) fusion(bf16[256,2688]{1,0:T(8,128)(2,1)} %get-tuple-element.30.x_ref.bc_ref, f32[40,2560]{1,0:T(8,128)S(1)} %copy-done.4, f32[40,256]{1,0:T(8,128)S(1)} %fusion.13, f32[256]{0:T(256)S(1)} %get-tuple-element.46, f32[40]{0:T(128)S(1)} %slice_reduce_fusion, ...), kind=kOutput, calls=%fused_computation.27 | convolution fusion | flops 316651520 | bytes 5715264 | tf_op jit(solution)/shard_map/dot_general | solution.py:32
  35.9 1.5 pad_maximum_fusion.1.parts_ref
  37.4 83.9 %exchange.1 = bf16[32,4,2560]{2,1,0:T(4,128)(2,1)} custom-call(bf16[32,4,2560]{2,1,0:T(4,128)(2,1)} %pad_maximum_fusion.1.parts_ref, f32[1,128]{1,0:T(1,128)} %pad_bitcast_fusion.decay_ref), custom_call_target="tpu_custom_call" | custom-call | tf_op jit(solution)/shard_map/exchange/pallas_call | solution.py:326
  121.3 2.5 %multiply_reduce_fusion.3 = f32[2560]{0:T(1024)} fusion(bf16[32,4,2560]{2,1,0:T(4,128)(2,1)} %exchange.1), kind=kLoop, calls=%fused_computation.42 | loop fusion | flops 652800 | bytes 665600 | tf_op jit(solution)/shard_map/reduce_sum | solution.py:404
  123.8 1.9 fusion.61
  126.3 2.9 %convolution_multiply_fusion = f32[256,2560]{1,0:T(8,128)} fusion(bf16[64,2560]{1,0:T(8,128)(2,1)S(1)} %reshape.99, bf16[256,2560]{1,0:T(8,128)(2,1)S(1)} %fusion, bf16[256,2688]{1,0:T(8,128)(2,1)} %get-tuple-element.30.x_ref.bc_ref), kind=kOutput, calls=%fused_computation | convolution fusion | flops 85196800 | bytes 4325376 | tf_op jit(solution)/shard_map/dot_general | solution.py:32
  129.3 1.3 fusion.23
  130.6 5.0 %fusion.65 = (f32[40]{0:T(128)}, f32[256,40]{0,1:T(8,128)}) fusion(f32[40,2560]{1,0:T(8,128)S(1)} %copy-done.4, f32[256,2560]{1,0:T(8,128)S(1)} %fusion.23, bf16[256,2560]{1,0:T(8,128)(2,1)} %copy-done), kind=kOutput, calls=%fused_computation.124 | convolution fusion | flops 315893728 | bytes 4382880 | tf_op jit(solution)/shard_map/dot_general | solution.py:32
  135.7 17.8 %core.1 = (bf16[256,2560]{1,0:T(8,128)(2,1)}, f32[20,4,256]{2,1,0:T(4,128)}, f32[20,1,128]{2,1,0:T(1,128)}, f32[256,128]{1,0:T(8,128)}) custom-call(bf16[256,2688]{1,0:T(8,128)(2,1)} %get-tuple-element.30.x_ref.bc_ref, bf16[256,2560]{1,0:T(8,128)(2,1)} %bitcast.117, bf16[256,2688]{1,0:T(8,128)(2,1)} %get-tuple-element.30.x_ref.bc_ref, ...), custom_call_target="tpu_custom_call" | custom-call | flops 1342177280 | bytes 5242880 | tf_op jit(solution)/shard_map/core/pallas_call | solution.py:100
  153.5 2.6 %add_convert_fusion.3 = (bf16[256,64]{1,0:T(8,128)(2,1)S(1)}, bf16[256,64]{1,0:T(8,128)(2,1)}) fusion(f32[256,64]{1,0:T(8,128)S(1)} %fusion.66, f32[256,128]{1,0:T(8,128)} %get-tuple-element.12, bf16[256,2560]{1,0:T(8,128)(2,1)} %copy-done, bf16[64,2560]{1,0:T(8,128)(2,1)S(1)} %reshape.98), kind=kOutput, calls=%fused_computation.48 | convolution fusion | flops 83951616 | bytes 1900544 | tf_op jit(solution)/shard_map/dot_general | solution.py:32
  156.1 3.5 %add_convert_fusion.2 = bf16[256,2560]{1,0:T(8,128)(2,1)} fusion(f32[256,2560]{1,0:T(8,128)S(1)} %fusion.23, f32[256,2560]{1,0:T(8,128)} %get-tuple-element.54, bf16[256,2560]{1,0:T(8,128)(2,1)S(1)} %copy-done.5), kind=kLoop, calls=%fused_computation.26 | loop fusion | flops 2621440 | bytes 7864320 | tf_op jit(solution)/shard_map/convert.3
  159.6 3.4 %concatenate.20 = bf16[256,2688]{1,0:T(8,128)(2,1)} concatenate(bf16[256,2560]{1,0:T(8,128)(2,1)} %add_convert_fusion.2, bf16[256,64]{1,0:T(8,128)(2,1)S(1)} %copy-done.6, bf16[256,64]{1,0:T(8,128)(2,1)S(1)} %get-tuple-element.38), dimensions={1} | concatenate | bytes 2752512 | tf_op jit(solution)/shard_map/concatenate | solution.py:401
  163.0 5.1 %fusion.57 = (f32[2688]{0:T(1024)S(1)}, f32[2688]{0:T(1024)S(1)}, f32[2688]{0:T(1024)S(1)}, f32[2688]{0:T(1024)S(1)}, f32[2688]{0:T(1024)S(1)}, /*index=5*/f32[256,2688]{1,0:T(8,128)S(1)}) fusion(bf16[1,256,2688]{2,1,0:T(8,128)(2,1)S(1)} %copy-done.2, bf16[256,2688]{1,0:T(8,128)(2,1)S(1)} %bitcast.116, bf16[3,2688]{1,0:T(4,128)(2,1)S(1)} %copy-done.17, ...), kind=kLoop, calls=%fused_computation.118 | loop fusion | flops 23382912 | bytes 9704448 | tf_op jit(solution)/shard_map/reduce_sum | solution.py:418
  169.4 2.0 add_convert_fusion
  172.3 2.4 %fusion.9 = f32[40,256]{1,0:T(8,128)S(1)} fusion(f32[40,2560]{1,0:T(8,128)S(1)} %copy-done.4, f32[256,2560]{1,0:T(8,128)S(1)} %copy-done.3, f32[256,40]{0,1:T(8,128)S(1)} %copy-done.7, f32[40,256]{1,0:T(8,128)S(1)} %reshape.101, f32[40,256]{1,0:T(8,128)S(1)} %reshape.100), kind=kOutput, calls=%fused_computation.37 | convolution fusion | flops 314603520 | bytes 3194880 | tf_op jit(solution)/shard_map/dot_general | solution.py:32
  176.8 33.2 %total.1 = f32[32,4,128]{2,1,0:T(4,128)} custom-call(f32[32,4,128]{2,1,0:T(4,128)} %bitcast.118), custom_call_target="tpu_custom_call" | custom-call | tf_op jit(solution)/shard_map/total/pallas_call | solution.py:225
  209.9 2.3 %collective-permute-start.1 = (bf16[3,2688]{1,0:T(4,128)(2,1)S(1)}, bf16[3,2688]{1,0:T(4,128)(2,1)S(1)}, u32[]{:S(2)}, u32[]{:S(2)}) collective-permute-start(bf16[3,2688]{1,0:T(4,128)(2,1)S(1)} %add_convert_fusion.5), channel_id=1, source_target_pairs={{16,0},{32,16},{48,32},{64,48},{80,64},{96,80},{112,96},{128,112},... | collective-permute-start | bytes 48392 | tf_op jit(solution)/shard_map/ppermute | solution.py:22
  212.3 1.4 fusion.63
  213.6 1.3 split.20
  216.4 2.8 %fusion.8 = bf16[1,256,2688]{2,1,0:T(8,128)(2,1)} fusion(bf16[259,2688]{1,0:T(8,128)(2,1)} %add_convert_fusion, bf16[3,2688]{1,0:T(4,128)(2,1)S(1)} %collective-permute-done.1), kind=kLoop, calls=%fused_computation.32 | loop fusion | flops 2752512 | bytes 2768640 | tf_op jit(solution)/shard_map/broadcast_in_dim | solution.py:431
  (140 shorter events, 20.1 us)
Async XLA Ops:
  0.6 21.6 %copy-start.1 = (bf16[1,256,2688]{2,1,0:T(8,128)(2,1)S(1)}, bf16[1,256,2688]{2,1,0:T(8,128)(2,1)}, u32[]{:S(2)}) copy-start(bf16[1,256,2688]{2,1,0:T(8,128)(2,1)} %param.10) | copy-start | bytes 4128772
  0.6 19.9 %copy-start.36 = (f32[40]{0:T(128)S(1)}, f32[40]{0:T(128)}, u32[]{:S(2)}) copy-start(f32[40]{0:T(128)} %param.16) | copy-start | bytes 484
  0.7 21.6 %copy-start.22 = (f32[2688]{0:T(1024)S(1)}, f32[2688]{0:T(1024)}, u32[]{:S(2)}) copy-start(f32[2688]{0:T(1024)} %param.13) | copy-start | bytes 32260
  1.6 20.7 %collective-permute-start = (bf16[3,2688]{1,0:T(4,128)(2,1)S(1)}, bf16[3,2688]{1,0:T(4,128)(2,1)S(1)}, u32[]{:S(2)}, u32[]{:S(2)}) collective-permute-start(bf16[3,2688]{1,0:T(4,128)(2,1)S(1)} %slice_bitcast_fusion), channel_id=1, source_target_pairs={{0,16},{16,32},{32,48},{48,64},{64,80},{80,96},{96,112},{112,128},... | collective-permute-start | bytes 48392 | tf_op jit(solution)/shard_map/ppermute | solution.py:22
  6.5 14.0 %copy-start.38 = (s32[256]{0:T(256)}, s32[256]{0:T(256)S(1)}, u32[]{:S(2)}) copy-start(s32[256]{0:T(256)S(1)} %iota_add_fusion) | copy-start | bytes 3076
  11.4 15.3 %copy-start.24 = (pred[256]{0:T(512)(128)(4,1)}, pred[256]{0:T(512)(128)(4,1)S(1)}, u32[]{:S(2)}) copy-start(pred[256]{0:T(512)(128)(4,1)S(1)} %get-tuple-element.48) | copy-start | bytes 772
  11.4 15.3 %copy-start.26 = (pred[256]{0:T(512)(128)(4,1)}, pred[256]{0:T(512)(128)(4,1)S(1)}, u32[]{:S(2)}) copy-start(pred[256]{0:T(512)(128)(4,1)S(1)} %get-tuple-element.49) | copy-start | bytes 772
  11.4 15.3 %copy-start.28 = (pred[256]{0:T(512)(128)(4,1)}, pred[256]{0:T(512)(128)(4,1)S(1)}, u32[]{:S(2)}) copy-start(pred[256]{0:T(512)(128)(4,1)S(1)} %get-tuple-element.50) | copy-start | bytes 772
  15.3 11.4 %copy-start.8 = (f32[2688]{0:T(1024)}, f32[2688]{0:T(1024)S(1)}, u32[]{:S(2)}) copy-start(f32[2688]{0:T(1024)S(1)} %get-tuple-element.23) | copy-start | bytes 32260
  15.3 11.4 %copy-start.10 = (f32[2688]{0:T(1024)}, f32[2688]{0:T(1024)S(1)}, u32[]{:S(2)}) copy-start(f32[2688]{0:T(1024)S(1)} %get-tuple-element.24) | copy-start | bytes 32260
  15.3 11.4 %copy-start.12 = (f32[2688]{0:T(1024)}, f32[2688]{0:T(1024)S(1)}, u32[]{:S(2)}) copy-start(f32[2688]{0:T(1024)S(1)} %get-tuple-element.25) | copy-start | bytes 32260
  15.3 11.4 %copy-start.14 = (f32[2688]{0:T(1024)}, f32[2688]{0:T(1024)S(1)}, u32[]{:S(2)}) copy-start(f32[2688]{0:T(1024)S(1)} %get-tuple-element.26) | copy-start | bytes 32260
  15.4 6.8 %copy-start.34 = (f32[40]{0:T(128)}, f32[40]{0:T(128)S(1)}, u32[]{:S(2)}) copy-start(f32[40]{0:T(128)S(1)} %exponential_multiply_fusion) | copy-start | bytes 484
  22.2 4.5 %copy-start.16 = (bf16[3,2688]{1,0:T(4,128)(2,1)}, bf16[3,2688]{1,0:T(4,128)(2,1)S(1)}, u32[]{:S(2)}) copy-start(bf16[3,2688]{1,0:T(4,128)(2,1)S(1)} %collective-permute-done) | copy-start | bytes 48388
  22.3 5.9 %copy-start.4 = (f32[40,2560]{1,0:T(8,128)S(1)}, f32[40,2560]{1,0:T(8,128)}, u32[]{:S(2)}) copy-start(f32[40,2560]{1,0:T(8,128)} %constant.40.clone) | copy-start | bytes 1228804
  22.3 5.9 %copy-start.18 = (bf16[1,256,40]{1,2,0:T(8,128)(2,1)S(1)}, bf16[1,256,40]{1,2,0:T(8,128)(2,1)}, u32[]{:S(2)}) copy-start(bf16[1,256,40]{1,2,0:T(8,128)(2,1)} %param.11) | copy-start | bytes 61444
  22.3 5.9 %copy-start.31 = (f32[40]{0:T(128)S(1)}, f32[40]{0:T(128)}, u32[]{:S(2)}) copy-start(f32[40]{0:T(128)} %param.14) | copy-start | bytes 484
  156.1 3.5 %copy-start.6 = (bf16[256,64]{1,0:T(8,128)(2,1)S(1)}, bf16[256,64]{1,0:T(8,128)(2,1)}, u32[]{:S(2)}) copy-start(bf16[256,64]{1,0:T(8,128)(2,1)} %get-tuple-element.39) | copy-start | bytes 98308
  163.0 5.2 %copy-start.9 = (f32[2688]{0:T(1024)S(1)}, f32[2688]{0:T(1024)}, u32[]{:S(2)}) copy-start(f32[2688]{0:T(1024)} %copy-done.8) | copy-start | bytes 32260
  163.0 5.2 %copy-start.11 = (f32[2688]{0:T(1024)S(1)}, f32[2688]{0:T(1024)}, u32[]{:S(2)}) copy-start(f32[2688]{0:T(1024)} %copy-done.10) | copy-start | bytes 32260
  163.0 5.2 %copy-start.13 = (f32[2688]{0:T(1024)S(1)}, f32[2688]{0:T(1024)}, u32[]{:S(2)}) copy-start(f32[2688]{0:T(1024)} %copy-done.12) | copy-start | bytes 32260
  163.0 5.2 %copy-start.15 = (f32[2688]{0:T(1024)S(1)}, f32[2688]{0:T(1024)}, u32[]{:S(2)}) copy-start(f32[2688]{0:T(1024)} %copy-done.14) | copy-start | bytes 32260
  171.4 4.5 %copy-start.37 = (f32[40]{0:T(128)S(1)}, f32[40]{0:T(128)}, u32[]{:S(2)}) copy-start(f32[40]{0:T(128)} %param.15) | copy-start | bytes 484
  209.9 6.5 %collective-permute-start.1 = (bf16[3,2688]{1,0:T(4,128)(2,1)S(1)}, bf16[3,2688]{1,0:T(4,128)(2,1)S(1)}, u32[]{:S(2)}, u32[]{:S(2)}) collective-permute-start(bf16[3,2688]{1,0:T(4,128)(2,1)S(1)} %add_convert_fusion.5), channel_id=1, source_target_pairs={{16,0},{32,16},{48,32},{64,48},{80,64},{96,80},{112,96},{128,112},... | collective-permute-start | bytes 48392 | tf_op jit(solution)/shard_map/ppermute | solution.py:22
  (20 other events, 56.6 us)

commit v2 on v1

--- a/solution.py
+++ b/solution.py
@@ -11,6 +11,7 @@
 N = 64
 DIN = H * P_SIZE
 PAIRS = H // 2
+EARLY, MIDDLE = 3, 12
 HIGHEST = lax.Precision.HIGHEST
 F32 = jnp.float32
 BF16 = jnp.bfloat16
@@ -34,27 +35,12 @@
     )
 
 
-def core_kernel(
-    x_ref, dy_ref, bc_ref, steps_ref, docc_ref, docr_ref, skip_ref,
-    dx_ref, rows_ref, xdy_ref, dbc_ref,
-    scores, masked, gacc,
-):
-    j = pl.program_id(0)
+def core_pair(j, x_ref, dy_ref, steps_ref, skip_ref, dx_ref, rows_ref, xdy_ref, scores, masked, gacc):
     length = x_ref.shape[0]
-
-    @pl.when(j == 0)
-    def _():
-        b, c = bc_ref[:, :N], bc_ref[:, N:]
-        scores[...] = dot(b, c, 1, 1)
-        s = lax.broadcasted_iota(jnp.int32, (length, length), 0)
-        t = lax.broadcasted_iota(jnp.int32, (length, length), 1)
-        same = (docc_ref[...] == docr_ref[...]) & (t >= s)
-        masked[...] = jnp.where(same, 0.0, -1e30)
-        gacc[...] = jnp.zeros_like(gacc)
-
-    x, dy = x_ref[...], dy_ref[...]
+    where = pl.ds(pl.multiple_of(j * 2 * P_SIZE, 2 * P_SIZE), 2 * P_SIZE)
+    x, dy = x_ref[:, where], dy_ref[:, where]
     lane = lax.broadcasted_iota(jnp.int32, (length, 2 * P_SIZE), 1)
-    rows = steps_ref[0]
+    rows = steps_ref[j]
     cols = rows.T
     mixes = []
     total = None
@@ -66,7 +52,7 @@
         w = ds * scores[...]
         part = dw * ds
         total = part if total is None else total + part
-        rows_ref[0, h + 2 : h + 3, :] = jnp.sum(dw * w, axis=0, keepdims=True)
+        rows_ref[j, h + 2 : h + 3, :] = jnp.sum(dw * w, axis=0, keepdims=True)
         mixes.append(dot(w.astype(BF16), dy, 1, 0))
     gacc[...] += total
     mix = jnp.where(lane < P_SIZE, mixes[0], mixes[1])
@@ -77,63 +63,196 @@
     head = lax.broadcasted_iota(jnp.int32, (8, 2 * P_SIZE), 0)
     pick = lax.broadcasted_iota(jnp.int32, (8, 2 * P_SIZE), 1) // P_SIZE == head
     pick = jnp.where(pick, 1.0, 0.0).astype(BF16)
-    rows_ref[0, :2, :] = (dot(pick, high, 1, 1) + dot(pick, low, 1, 1))[:2]
-    xdy_ref[0] = jnp.sum(xf * dyf, axis=0, keepdims=True)
-    dx_ref[...] = (mix + skip_ref[0] * dyf).astype(BF16)
-
-    @pl.when(j == PAIRS - 1)
-    def _():
-        b, c = bc_ref[:, :N], bc_ref[:, N:]
-        g = gacc[...].astype(BF16)
-        dbc_ref[:, :N] = dot(g, c, 1, 0)
-        dbc_ref[:, N:] = dot(g, b, 0, 0)
-
-
-def core(activated, dy, cum, step, docs, skip_wide):
+    rows_ref[j, :2, :] = (dot(pick, high, 1, 1) + dot(pick, low, 1, 1))[:2]
+    xdy_ref[j] = jnp.sum(xf * dyf, axis=0, keepdims=True)
+    dx_ref[:, where] = (mix + skip_ref[j] * dyf).astype(BF16)
+
+
+def core_kernel(
+    x_ref, dy_ref, steps_ref, docc_ref, docr_ref, skip_ref, parts_ref, decay_ref,
+    dx_ref, rows_ref, xdy_ref, dbc_ref, out_ref,
+    scores, masked, gacc,
+    other, theirs, comb, chain, got, chains, turned, result, lend, landed,
+    pair_sems, send_a, recv_a, send_d, recv_d, send_b, recv_b,
+):
+    length = x_ref.shape[0]
+    nc = lax.axis_size("ctx")
+    chips = nc // 2
+    ctx = lax.axis_index("ctx")
+    chip, side = ctx // 2, lax.rem(ctx, 2)
+    partner = chip * 2 + 1 - side
+    mesh = pl.DeviceIdType.MESH
+    rows = parts_ref.shape[2] // 2
+
+    def target(k):
+        return lax.rem(chip + k, chips)
+
+    def peer(k):
+        return target(k) * 2 + side
+
+    def send(src, dst, sends, recvs, k):
+        return pltpu.make_async_remote_copy(
+            src_ref=src, dst_ref=dst, send_sem=sends.at[k], recv_sem=recvs.at[k],
+            device_id={"ctx": peer(k)}, device_id_type=mesh,
+        )
+
+    def swap(src, dst, i):
+        return pltpu.make_async_remote_copy(
+            src_ref=src, dst_ref=dst, send_sem=pair_sems.at[2 * i], recv_sem=pair_sems.at[2 * i + 1],
+            device_id={"ctx": partner}, device_id_type=mesh,
+        )
+
+    def both_ways(i):
+        half = (i + 1) // 2
+        return jnp.where(lax.rem(i, 2) == 1, half, chips - half)
+
+    def pairs(start, stop):
+        @pl.loop(start, stop)
+        def _(j):
+            core_pair(
+                j, x_ref, dy_ref, steps_ref, skip_ref, dx_ref, rows_ref, xdy_ref,
+                scores, masked, gacc,
+            )
+
+    barrier = pltpu.get_barrier_semaphore()
+    pl.semaphore_signal(barrier, 1, device_id={"ctx": partner}, device_id_type=mesh)
+
+    @pl.loop(1, chips)
+    def _(k):
+        pl.semaphore_signal(barrier, 1, device_id={"ctx": peer(k)}, device_id_type=mesh)
+
+    b, c = x_ref[:, DIN : DIN + N], x_ref[:, DIN + N :]
+    scores[...] = dot(b, c, 1, 1)
+    s = lax.broadcasted_iota(jnp.int32, (length, length), 0)
+    t = lax.broadcasted_iota(jnp.int32, (length, length), 1)
+    same = (docc_ref[...] == docr_ref[...]) & (t >= s)
+    masked[...] = jnp.where(same, 0.0, -1e30)
+    gacc[...] = jnp.zeros_like(gacc)
+    pairs(0, EARLY)
+    pl.semaphore_wait(barrier, chips)
+
+    gives = swap(parts_ref.at[1 - side], other, 0)
+    tells = swap(decay_ref, theirs, 1)
+    gives.start()
+    tells.start()
+    gives.wait()
+    tells.wait()
+
+    shape = (128, parts_ref.shape[3])
+    head = lax.broadcasted_iota(jnp.int32, shape, 1) // P_SIZE + side * (H // 2)
+    own = jnp.where(head == lax.broadcasted_iota(jnp.int32, shape, 0), 1.0, 0.0)
+    mine, yours = decay_ref[...], theirs[...]
+    stacked = jnp.concatenate([jnp.broadcast_to(mine, (8, 128)), jnp.broadcast_to(yours, (8, 128))])
+    spread = dot(stacked, own, 1, 0, HIGHEST)
+    mine_wide, yours_wide = spread[:8], spread[8:]
+    is_forward = lax.broadcasted_iota(jnp.int32, (2 * rows, shape[1]), 0) < rows
+    keep_other = is_forward == (side == 0)
+    own_gain = jnp.where(keep_other, yours_wide, 1.0)
+    other_gain = jnp.where(keep_other, 1.0, mine_wide)
+    for i in range(chips):
+        comb[i] = (
+            own_gain * parts_ref[side, i].astype(F32) + other_gain * other[i].astype(F32)
+        ).astype(BF16)
+    chain[...] = mine * yours
+
+    def out(k):
+        return send(comb.at[target(k)], got.at[chip], send_a, recv_a, k)
+
+    def small(k):
+        return send(chain, chains.at[chip], send_d, recv_d, k)
+
+    def back(k):
+        return send(turned.at[target(k)], result.at[chip], send_b, recv_b, k)
+
+    @pl.loop(1, chips)
+    def _(i):
+        small(both_ways(i)).start()
+        out(both_ways(i)).start()
+
+    got[chip] = comb[chip]
+    chains[chip] = chain[...]
+    pairs(EARLY, MIDDLE)
+
+    @pl.loop(1, chips)
+    def _(k):
+        small(k).wait()
+        out(k).wait()
+
+    decay = dot(chains[:, 0, :], own, 1, 0, HIGHEST)
+    forward = jnp.zeros((rows, shape[1]), F32)
+    for i in range(chips):
+        turned[i, :rows] = forward.astype(BF16)
+        forward = decay[i : i + 1] * forward + got[i, :rows].astype(F32)
+    backward = jnp.zeros((rows, shape[1]), F32)
+    for i in reversed(range(chips)):
+        turned[i, rows:] = backward.astype(BF16)
+        backward = decay[i : i + 1] * backward + got[i, rows:].astype(F32)
+
+    @pl.loop(1, chips)
+    def _(i):
+        back(both_ways(i)).start()
+
+    result[chip] = turned[chip]
+    pairs(MIDDLE, PAIRS)
+    g = gacc[...].astype(BF16)
+    dbc_ref[:, :N] = dot(g, c, 1, 0)
+    dbc_ref[:, N:] = dot(g, b, 0, 0)
+
+    @pl.loop(1, chips)
+    def _(k):
+        back(k).wait()
+
+    for i in range(chips):
+        value = result[i].astype(F32)
+        here = jnp.where(keep_other, 1.0, yours_wide) * value
+        here = here + jnp.where(keep_other, 0.0, other[i].astype(F32))
+        there = jnp.where(keep_other, mine_wide, 1.0) * value
+        there = there + jnp.where(keep_other, parts_ref[side, i].astype(F32), 0.0)
+        out_ref[side, i] = here.astype(BF16)
+        lend[i] = there.astype(BF16)
+    lends = swap(lend, landed, 2)
+    lends.start()
+    lends.wait()
+    out_ref[1 - side] = landed[...]
+
+
+def core(activated, dy, cum, step, docs, skip_wide, parts, decay):
     length = activated.shape[0]
+    chips = parts.shape[1]
     pairs = lambda v: v.reshape(PAIRS, 2, length)
     packed = jnp.concatenate(
         [pairs(cum), pairs(step), jnp.zeros((PAIRS, 4, length), F32)], axis=1
     )
-    wide = pl.BlockSpec((length, 2 * P_SIZE), lambda j: (0, j))
-    lanes = pl.BlockSpec((1, 1, 2 * P_SIZE), lambda j: (j, 0, 0))
-    dx, rows, xdy, dbc = pl.pallas_call(
+    vmem = pl.BlockSpec(memory_space=pltpu.VMEM)
+    dma = pltpu.SemaphoreType.DMA
+    half = pltpu.VMEM(parts.shape[1:], BF16)
+    line = pltpu.VMEM((1, 128), F32)
+    dx, rows, xdy, dbc, carried = pl.pallas_call(
         core_kernel,
-        grid=(PAIRS,),
-        in_specs=[
-            wide,
-            wide,
-            pl.BlockSpec((length, 2 * N), lambda j: (0, PAIRS)),
-            pl.BlockSpec((1, 8, length), lambda j: (j, 0, 0)),
-            pl.BlockSpec((length, 1), lambda j: (0, 0)),
-            pl.BlockSpec((1, length), lambda j: (0, 0)),
-            lanes,
-        ],
-        out_specs=[
-            wide,
-            pl.BlockSpec((1, 4, length), lambda j: (j, 0, 0)),
-            lanes,
-            pl.BlockSpec((length, 2 * N), lambda j: (0, 0)),
-        ],
+        in_specs=[vmem] * 8,
+        out_specs=[vmem] * 5,
         out_shape=[
             jax.ShapeDtypeStruct((length, DIN), BF16),
             jax.ShapeDtypeStruct((PAIRS, 4, length), F32),
             jax.ShapeDtypeStruct((PAIRS, 1, 2 * P_SIZE), F32),
             jax.ShapeDtypeStruct((length, 2 * N), F32),
+            jax.ShapeDtypeStruct(parts.shape, BF16),
         ],
-        scratch_shapes=[pltpu.VMEM((length, length), F32)] * 3,
-        cost_estimate=pl.CostEstimate(
-            flops=4 * H * length * length * 2 * P_SIZE,
-            bytes_accessed=8 * length * DIN,
-            transcendentals=H * length * length,
-        ),
+        scratch_shapes=[
+            *[pltpu.VMEM((length, length), F32)] * 3,
+            half, line, half, line, half, pltpu.VMEM((chips, 1, 128), F32),
+            half, half, half, half,
+            dma((6,)), *[dma((chips,))] * 6,
+        ],
+        compiler_params=pltpu.CompilerParams(collective_id=1, has_side_effects=True),
         name="core",
     )(
-        activated, dy, activated, packed,
-        docs[:, None], docs[None, :], skip_wide.reshape(PAIRS, 1, 2 * P_SIZE),
+        activated, dy, packed, docs[:, None], docs[None, :],
+        skip_wide.reshape(PAIRS, 1, 2 * P_SIZE), parts,
+        jnp.pad(decay, (0, 128 - H))[None, :],
     )
     xdx, col = rows[:, :2].reshape(H, length), rows[:, 2:].reshape(H, length)
-    return dx, xdx, col, xdy, dbc
+    return dx, xdx, col, xdy, dbc, carried
 
 
 def total_kernel(
@@ -241,114 +360,21 @@
     return summed.reshape(-1)[: vector.shape[0]]
 
 
-def exchange_kernel(
-    parts_ref, decay_ref, out_ref, got, decays, turned, result,
-    send_a, recv_a, send_d, recv_d, send_b, recv_b,
-):
-    nc = lax.axis_size("ctx")
-    ctx = lax.axis_index("ctx")
-    rows = parts_ref.shape[1] // 2
-
-    def peer(k):
-        return lax.rem(ctx + k, nc)
-
-    def send(src, dst, sends, recvs, k):
-        return pltpu.make_async_remote_copy(
-            src_ref=src, dst_ref=dst, send_sem=sends.at[k], recv_sem=recvs.at[k],
-            device_id={"ctx": peer(k)}, device_id_type=pl.DeviceIdType.MESH,
-        )
-
-    def both_ways(i):
-        half = (i + 1) // 2
-        return jnp.where(lax.rem(i, 2) == 1, half, nc - half)
-
-    barrier = pltpu.get_barrier_semaphore()
-
-    @pl.loop(1, nc)
-    def _(k):
-        pl.semaphore_signal(
-            barrier, 1, device_id={"ctx": peer(k)}, device_id_type=pl.DeviceIdType.MESH
-        )
-
-    pl.semaphore_wait(barrier, nc - 1)
-
-    def small(k):
-        return send(decay_ref, decays.at[ctx], send_d, recv_d, k)
-
-    def out(k):
-        return send(parts_ref.at[peer(k)], got.at[ctx], send_a, recv_a, k)
-
-    def back(k):
-        return send(turned.at[peer(k)], result.at[ctx], send_b, recv_b, k)
-
-    @pl.loop(1, nc)
-    def _(i):
-        small(both_ways(i)).start()
-        out(both_ways(i)).start()
-
-    decays[ctx] = decay_ref[...]
-    got[ctx] = parts_ref[ctx]
-
-    @pl.loop(1, nc)
-    def _(k):
-        small(k).wait()
-        out(k).wait()
-
-    shape = (128, parts_ref.shape[2])
-    head = lax.broadcasted_iota(jnp.int32, shape, 1) // P_SIZE
-    own = head == lax.broadcasted_iota(jnp.int32, shape, 0)
-    decay = dot(decays[:, 0, :], jnp.where(own, 1.0, 0.0), 1, 0, HIGHEST)
-    forward = jnp.zeros((rows, parts_ref.shape[2]), F32)
-    for b in range(nc):
-        turned[b, :rows] = forward.astype(BF16)
-        forward = decay[b : b + 1] * forward + got[b, :rows].astype(F32)
-    backward = jnp.zeros((rows, parts_ref.shape[2]), F32)
-    for b in reversed(range(nc)):
-        turned[b, rows:] = backward.astype(BF16)
-        backward = decay[b : b + 1] * backward + got[b, rows:].astype(F32)
-
-    @pl.loop(1, nc)
-    def _(i):
-        back(both_ways(i)).start()
-
-    result[ctx] = turned[ctx]
-
-    @pl.loop(1, nc)
-    def _(k):
-        back(k).wait()
-
-    out_ref[...] = result[...]
-
-
-def exchange(parts, decay):
-    nc = parts.shape[0]
-    dma = pltpu.SemaphoreType.DMA
-    return pl.pallas_call(
-        exchange_kernel,
-        out_shape=jax.ShapeDtypeStruct(parts.shape, BF16),
-        in_specs=[pl.BlockSpec(memory_space=pltpu.VMEM)] * 2,
-        out_specs=pl.BlockSpec(memory_space=pltpu.VMEM),
-        scratch_shapes=[
-            pltpu.VMEM(parts.shape, BF16),
-            pltpu.VMEM((nc, 1, 128), F32),
-            pltpu.VMEM(parts.shape, BF16),
-            pltpu.VMEM(parts.shape, BF16),
-            *[dma((nc,))] * 6,
-        ],
-        compiler_params=pltpu.CompilerParams(collective_id=1, has_side_effects=True),
-        name="exchange",
-    )(parts, jnp.pad(decay, (0, 128 - H))[None, :])
-
-
 def per_device(xbc, dt_raw, conv_weight, conv_bias, dt_bias, a_log, d_skip, grad_out, doc_lengths):
     taps = conv_weight.shape[0]
     own_rows = xbc[0]
     length = own_rows.shape[0]
     count = lax.axis_size("ctx")
     dy = grad_out[0]
-    expand = jnp.asarray(np.kron(np.eye(H), np.ones((1, P_SIZE))), F32)
-    widen = lambda v: dot(v, expand, 0, 0, HIGHEST)
-    narrow = lambda v: dot(expand, v, 1, 1, HIGHEST)
+    expand = jnp.asarray(np.kron(np.eye(H), np.ones((1, P_SIZE))), BF16)
+    twice = jnp.concatenate([expand, expand])
+
+    def halves(v):
+        high = lax.reduce_precision(v, 8, 7)
+        return high.astype(BF16), (v - high).astype(BF16)
+
+    widen = lambda v: dot(jnp.concatenate(halves(v)), twice, 0, 0)
+    narrow = lambda v: sum(dot(expand, part, 1, 1) for part in halves(v))
     upto = jnp.triu(jnp.ones((length, length), F32))
 
     offset = lax.axis_index("ctx") * length
@@ -383,15 +409,16 @@
     local = dot(b, weighted, 0, 0)
     seeded = dot(c, led, 0, 0)
 
-    rows = N // count
-    parts = jnp.concatenate(
-        [local.reshape(count, rows, DIN), seeded.reshape(count, rows, DIN)], axis=1
-    ).astype(BF16)
-    carried = exchange(parts, decay)
-    incoming = carried[:, :rows].reshape(N, DIN)
-    adjoint = carried[:, rows:].reshape(N, DIN)
-
-    dx, xdx, col, xdy, dbc = core(activated, dy, cum, step, docs, jnp.repeat(d_skip, P_SIZE))
+    chips = count // 2
+    rows = N // chips
+    split = lambda v: v.astype(BF16).reshape(chips, rows, 2, DIN // 2).transpose(2, 0, 1, 3)
+    parts = jnp.concatenate([split(local), split(seeded)], axis=2)
+    dx, xdx, col, xdy, dbc, carried = core(
+        activated, dy, cum, step, docs, jnp.repeat(d_skip, P_SIZE), parts, decay
+    )
+    join = lambda v: v.transpose(1, 2, 0, 3).reshape(N, DIN)
+    incoming, adjoint = join(carried[:, :, :rows]), join(carried[:, :, rows:])
+
     outer = dot(c, incoming, 1, 0)
     spread = dot(b, adjoint, 1, 0)
     from_lead = narrow(led.astype(F32) * outer)

time: 221 us -> 172 us (0.78)
  Pallas kernels: 135 us -> 90.9 us
  matrix products: 28.9 us -> 22.2 us
    pallas_call x2 -> x1, Pallas kernels: 102 us -> 55.2 us  [core(): pl.pallas_call(core_kernel, in_specs=[vmem] * 8, out_specs=[vmem] * 5, ou...]
    dot_general x13 -> x18, matrix products: 28.9 us -> 22.2 us  [dot(): lax.dot_general(a, b, (((ca,), (cb,)), ((), ())), precision=precision, pr...]
    convert_element_type x1, other arithmetic: 4.4 us -> 7.46 us  [per_device(): activated = jax.nn.silu(pre).astype(BF16)]
    pallas_call x1, Pallas kernels: 33.2 us -> 35.8 us  [total_sum(): pl.pallas_call(total_kernel, out_shape=jax.ShapeDtypeStruct(padded.shape,...]
    transpose x0 -> x4, local copies, waits for them, and re-layouts: none -> 2.47 us  [the longest x3 2.22 us: per_device(): join = lambda v: v.transpose(1, 2, 0, 3).reshape(N, DIN)]
  transfers between devices with their start and end apart: 2 -> 2, of which waited for: 0 -> 0; matrix products, arithmetic and copies ran while one was open for 8% -> 11% of each run, Pallas kernels for 0% -> 0%
where the time goes in v2:
time: 172 us; the launch traced here: 171 us
  Pallas kernels  90.9 us (53%)
  other arithmetic  29.2 us (17%)
  matrix products  22.2 us (13%)
  local copies, waits for them, and re-layouts  18.6 us (11%)
  starting transfers between devices  7.25 us (4%)
  between operations  2.72 us (2%)
    pallas_call x1, Pallas kernels, core(): pl.pallas_call(core_kernel, in_specs=[vmem] * 8, out_specs=[vmem] * 5, ou...  55.2 us
    pallas_call x1, Pallas kernels, total_sum(): pl.pallas_call(total_kernel, out_shape=jax.ShapeDtypeStruct(padded.shape,...  35.8 us
    dot_general x18, matrix products, dot(): lax.dot_general(a, b, (((ca,), (cb,)), ((), ())), precision=precision, pr...  22.2 us
    convert_element_type x1, other arithmetic, per_device(): activated = jax.nn.silu(pre).astype(BF16)  7.46 us
    reduce_sum x1, other arithmetic, per_device(): grad_bias = jnp.sum(grad_pre, axis=0)  7.32 us
    ppermute x2, starting transfers between devices, from_behind(): lax.ppermute(value, axis, [(source, source + steps) for source in range(l...  7.25 us
    split x3, local copies, waits for them, and re-layouts, per_device(): jnp.split(total, ends)  3.48 us
  transfers between devices with their start and end apart: 2, of which 0 were waited for; matrix products, arithmetic and copies ran while one was open for 11% of the time, Pallas kernels for 0%

profile of v2, /device:TPU:1, one launch (start us, length us, event | category | flops | bytes accessed | tf_op | source)
XLA Modules:
  0.0 170.9 jit_solution(16748369632524470047)
XLA Ops:
  1.5 4.9 %collective-permute-start = (bf16[3,2688]{1,0:T(4,128)(2,1)S(1)}, bf16[3,2688]{1,0:T(4,128)(2,1)S(1)}, u32[]{:S(2)}, u32[]{:S(2)}) collective-permute-start(bf16[3,2688]{1,0:T(4,128)(2,1)S(1)} %slice_bitcast_fusion.2), channel_id=1, source_target_pairs={{0,16},{16,32},{32,48},{48,64},{64,80},{80,96},{96,112},{112,128},... | collective-permute-start | bytes 48392 | tf_op jit(solution)/shard_map/ppermute | solution.py:23
  9.9 1.4 compare_convert_fusion.1
  15.3 3.2 %fusion.56 = f32[256,2560]{1,0:T(8,128)} fusion(bf16[40,2560]{1,0:T(8,128)(2,1)} %constant.40.clone, f32[40,256]{1,0:T(8,128)S(1)} %fusion.24, f32[256]{0:T(256)S(1)} %get-tuple-element.50, f32[40]{0:T(128)S(1)} %slice_reduce_fusion, bf16[1,256,40]{1,2,0:T(8,128)(2,1)} %param.11, f32[40]{0:T(128)} %param.14), kind=kOutput, calls=%fused_computation.110 | convolution fusion | flops 52561920 | bytes 2889024 | tf_op jit(solution)/shard_map/dot_general | solution.py:33
  22.8 7.5 %multiply_convert_fusion = (bf16[256,2688]{1,0:T(8,128)(2,1)S(1)}, f32[256,2688]{1,0:T(8,128)}) fusion(bf16[256,2688]{1,0:T(8,128)(2,1)} %bitcast.154, f32[2688]{0:T(1024)S(1)} %get-tuple-element.27, bf16[3,2688]{1,0:T(4,128)(2,1)S(1)} %collective-permute-done, pred[256]{0:T(512)(128)(4,1)S(1)} %get-tuple-element.52, f32[2688]{0:T(1024)S(1)} %get-tuple-element.28, ...), kind=kLoop, calls=%fused_computation.24 | loop fusion | flops 19955712 | bytes 5575680 | tf_op jit(solution)/shard_map/convert_element_type | solution.py:394
  30.8 3.9 %multiply_convert_fusion.1 = (bf16[256,2560]{1,0:T(8,128)(2,1)S(1)}, f32[256,2560]{1,0:T(8,128)}) fusion(bf16[256,2688]{1,0:T(8,128)(2,1)S(1)} %get-tuple-element.32.x_ref, f32[256,2560]{1,0:T(8,128)} %fusion.56, bf16[40,2560]{1,0:T(8,128)(2,1)S(1)} %copy-done.4, f32[256]{0:T(256)S(1)} %get-tuple-element.50, f32[40,256]{1,0:T(8,128)} %copy-done.9, ...), kind=kOutput, calls=%fused_computation.33 | convolution fusion | flops 55193600 | bytes 8131904 | tf_op jit(solution)/shard_map/dot_general | solution.py:33
  34.8 1.2 copy-done
  36.6 1.2 pad_maximum_fusion.1.parts_ref
  37.8 55.2 %core.1 = (bf16[256,2560]{1,0:T(8,128)(2,1)}, f32[20,4,256]{2,1,0:T(4,128)}, f32[20,1,128]{2,1,0:T(1,128)}, f32[256,128]{1,0:T(8,128)}, bf16[2,16,8,1280]{3,2,1,0:T(8,128)(2,1)}) custom-call(bf16[256,2688]{1,0:T(8,128)(2,1)} %copy-done.3, bf16[256,2560]{1,0:T(8,128)(2,1)} %bitcast.156, f32[20,8,256]{2,1,0:T(8,128)} %maximum_maximum_fusion.steps_ref, ...), custom_call_target="tpu_custom_call" | custom-call | tf_op jit(solution)/shard_map/core/pallas_call | solution.py:230
  93.0 1.6 multiply_reduce_fusion.3
  94.6 1.5 slice_bitcast_fusion
  97.0 2.9 %convolution_multiply_fusion = f32[256,2560]{1,0:T(8,128)} fusion(bf16[64,2560]{1,0:T(8,128)(2,1)S(1)} %bitcast.158, bf16[256,2560]{1,0:T(8,128)(2,1)S(1)} %fusion.1, bf16[256,2688]{1,0:T(8,128)(2,1)} %copy-done.3), kind=kOutput, calls=%fused_computation | convolution fusion | flops 85196800 | bytes 4325376 | tf_op jit(solution)/shard_map/dot_general | solution.py:33
  100.3 1.3 fusion.34
  103.8 1.7 %add_convert_fusion.2 = bf16[256,2560]{1,0:T(8,128)(2,1)} fusion(f32[256,2560]{1,0:T(8,128)S(1)} %fusion.34, f32[256,2560]{1,0:T(8,128)S(1)} %copy-done.5, bf16[256,2560]{1,0:T(8,128)(2,1)S(1)} %copy-done.8), kind=kLoop, calls=%fused_computation.32 | loop fusion | flops 2621440 | bytes 7864320 | tf_op jit(solution)/shard_map/convert.3
  105.6 3.3 %concatenate.31 = bf16[256,2688]{1,0:T(8,128)(2,1)} concatenate(bf16[256,2560]{1,0:T(8,128)(2,1)} %add_convert_fusion.2, bf16[256,64]{1,0:T(8,128)(2,1)S(1)} %get-tuple-element.41, bf16[256,64]{1,0:T(8,128)(2,1)S(1)} %get-tuple-element.40), dimensions={1} | concatenate | bytes 2752512 | tf_op jit(solution)/shard_map/concatenate | solution.py:428
  108.9 7.3 %fusion.67 = (f32[2688]{0:T(1024)S(1)}, f32[2688]{0:T(1024)S(1)}, f32[2688]{0:T(1024)S(1)}, f32[2688]{0:T(1024)S(1)}, f32[2688]{0:T(1024)S(1)}, /*index=5*/f32[256,2688]{1,0:T(8,128)S(1)}) fusion(bf16[1,256,2688]{2,1,0:T(8,128)(2,1)} %param.10, bf16[256,2688]{1,0:T(8,128)(2,1)} %bitcast.155, bf16[3,2688]{1,0:T(4,128)(2,1)S(1)} %copy-done.21, ...), kind=kLoop, calls=%fused_computation.142 | loop fusion | flops 23382912 | bytes 9704448 | tf_op jit(solution)/shard_map/reduce_sum | solution.py:445
  117.4 2.0 %add_convert_fusion = bf16[259,2688]{1,0:T(8,128)(2,1)} fusion(f32[256,2688]{1,0:T(8,128)S(1)} %get-tuple-element.35, f32[256,2688]{1,0:T(8,128)S(1)} %get-tuple-element.36, f32[256,2688]{1,0:T(8,128)S(1)} %get-tuple-element.37, f32[256,2688]{1,0:T(8,128)S(1)} %get-tuple-element.34), kind=kLoop, calls=%fused_computation.13 | loop fusion | flops 2784768 | bytes 12402432 | tf_op jit(solution)/shard_map/convert_element_type | solution.py:450
  120.0 2.3 %fusion.9 = f32[256,40]{0,1:T(8,128)S(1)} fusion(bf16[40,2560]{1,0:T(8,128)(2,1)S(1)} %copy-done.4, f32[256,2560]{1,0:T(8,128)} %convolution_multiply_fusion), kind=kOutput, calls=%fused_computation.41 | convolution fusion | flops 54394880 | bytes 2867200 | tf_op jit(solution)/shard_map/dot_general | solution.py:33
  122.4 2.1 %fusion.74 = (f32[40]{0:T(128)S(1)}, f32[256,40]{0,1:T(8,128)S(1)}) fusion(f32[256,40]{0,1:T(8,128)S(1)} %fusion.13, bf16[40,2560]{1,0:T(8,128)(2,1)S(1)} %copy-done.4, f32[256,2560]{1,0:T(8,128)S(1)} %fusion.34, bf16[256,2560]{1,0:T(8,128)(2,1)} %copy-done), kind=kOutput, calls=%fused_computation.147 | convolution fusion | flops 55070680 | bytes 4219040 | tf_op jit(solution)/shard_map/dot_general | solution.py:33
  125.3 1.1 fusion.68
  127.2 35.8 %total.1 = f32[32,4,128]{2,1,0:T(4,128)} custom-call(f32[32,4,128]{2,1,0:T(4,128)} %bitcast.163), custom_call_target="tpu_custom_call" | custom-call | tf_op jit(solution)/shard_map/total/pallas_call | solution.py:344
  163.0 2.3 %collective-permute-start.1 = (bf16[3,2688]{1,0:T(4,128)(2,1)S(1)}, bf16[3,2688]{1,0:T(4,128)(2,1)S(1)}, u32[]{:S(2)}, u32[]{:S(2)}) collective-permute-start(bf16[3,2688]{1,0:T(4,128)(2,1)S(1)} %add_convert_fusion.5), channel_id=1, source_target_pairs={{16,0},{32,16},{48,32},{64,48},{80,64},{96,80},{112,96},{128,112},... | collective-permute-start | bytes 48392 | tf_op jit(solution)/shard_map/ppermute | solution.py:23
  165.3 1.4 fusion.72
  166.7 1.3 split.20
  169.4 1.4 fusion.8
  (150 shorter events, 20.4 us)
Async XLA Ops:
  0.6 17.9 %copy-start.4 = (bf16[40,2560]{1,0:T(8,128)(2,1)S(1)}, bf16[40,2560]{1,0:T(8,128)(2,1)}, u32[]{:S(2)}) copy-start(bf16[40,2560]{1,0:T(8,128)(2,1)} %constant.40.clone) | copy-start | bytes 614404
  1.5 21.2 %collective-permute-start = (bf16[3,2688]{1,0:T(4,128)(2,1)S(1)}, bf16[3,2688]{1,0:T(4,128)(2,1)S(1)}, u32[]{:S(2)}, u32[]{:S(2)}) collective-permute-start(bf16[3,2688]{1,0:T(4,128)(2,1)S(1)} %slice_bitcast_fusion.2), channel_id=1, source_target_pairs={{0,16},{16,32},{32,48},{48,64},{64,80},{80,96},{96,112},{112,128},... | collective-permute-start | bytes 48392 | tf_op jit(solution)/shard_map/ppermute | solution.py:23
  6.4 5.5 %copy-start.38 = (s32[256]{0:T(256)}, s32[256]{0:T(256)S(1)}, u32[]{:S(2)}) copy-start(s32[256]{0:T(256)S(1)} %iota_add_fusion) | copy-start | bytes 3076
  11.3 11.4 %copy-start.26 = (pred[256]{0:T(512)(128)(4,1)}, pred[256]{0:T(512)(128)(4,1)S(1)}, u32[]{:S(2)}) copy-start(pred[256]{0:T(512)(128)(4,1)S(1)} %get-tuple-element.52) | copy-start | bytes 772
  11.3 11.4 %copy-start.28 = (pred[256]{0:T(512)(128)(4,1)}, pred[256]{0:T(512)(128)(4,1)S(1)}, u32[]{:S(2)}) copy-start(pred[256]{0:T(512)(128)(4,1)S(1)} %get-tuple-element.53) | copy-start | bytes 772
  11.3 11.4 %copy-start.30 = (pred[256]{0:T(512)(128)(4,1)}, pred[256]{0:T(512)(128)(4,1)S(1)}, u32[]{:S(2)}) copy-start(pred[256]{0:T(512)(128)(4,1)S(1)} %get-tuple-element.54) | copy-start | bytes 772
  12.0 7.1 %copy-start.40 = (f32[40]{0:T(128)}, f32[40]{0:T(128)S(1)}, u32[]{:S(2)}) copy-start(f32[40]{0:T(128)S(1)} %exponential_negate_fusion) | copy-start | bytes 484
  13.1 6.1 %copy-start.9 = (f32[40,256]{1,0:T(8,128)}, f32[40,256]{1,0:T(8,128)S(1)}, u32[]{:S(2)}) copy-start(f32[40,256]{1,0:T(8,128)S(1)} %fusion.24) | copy-start | bytes 122884
  13.3 5.8 %copy-start.33 = (f32[40]{0:T(128)}, f32[40]{0:T(128)S(1)}, u32[]{:S(2)}) copy-start(f32[40]{0:T(128)S(1)} %slice_reduce_fusion) | copy-start | bytes 484
  15.2 7.5 %copy-start.12 = (f32[2688]{0:T(1024)}, f32[2688]{0:T(1024)S(1)}, u32[]{:S(2)}) copy-start(f32[2688]{0:T(1024)S(1)} %get-tuple-element.25) | copy-start | bytes 32260
  15.3 7.5 %copy-start.14 = (f32[2688]{0:T(1024)}, f32[2688]{0:T(1024)S(1)}, u32[]{:S(2)}) copy-start(f32[2688]{0:T(1024)S(1)} %get-tuple-element.26) | copy-start | bytes 32260
  15.3 7.5 %copy-start.16 = (f32[2688]{0:T(1024)}, f32[2688]{0:T(1024)S(1)}, u32[]{:S(2)}) copy-start(f32[2688]{0:T(1024)S(1)} %get-tuple-element.27) | copy-start | bytes 32260
  15.3 7.5 %copy-start.18 = (f32[2688]{0:T(1024)}, f32[2688]{0:T(1024)S(1)}, u32[]{:S(2)}) copy-start(f32[2688]{0:T(1024)S(1)} %get-tuple-element.28) | copy-start | bytes 32260
  15.3 5.1 %copy-start.36 = (f32[40]{0:T(128)}, f32[40]{0:T(128)S(1)}, u32[]{:S(2)}) copy-start(f32[40]{0:T(128)S(1)} %exponential_multiply_fusion.1) | copy-start | bytes 484
  15.3 3.8 %copy-start.7 = (bf16[1,256,2560]{2,1,0:T(8,128)(2,1)S(1)}, bf16[1,256,2560]{2,1,0:T(8,128)(2,1)}, u32[]{:S(2)}) copy-start(bf16[1,256,2560]{2,1,0:T(8,128)(2,1)} %param.17) | copy-start | bytes 3932164
  21.1 9.2 %copy-start.25 = (s32[256]{0:T(256)}, s32[256]{0:T(256)S(1)}, u32[]{:S(2)}) copy-start(s32[256]{0:T(256)S(1)} %slice.97) | copy-start | bytes 3076
  22.7 7.5 %copy-start.20 = (bf16[3,2688]{1,0:T(4,128)(2,1)}, bf16[3,2688]{1,0:T(4,128)(2,1)S(1)}, u32[]{:S(2)}) copy-start(bf16[3,2688]{1,0:T(4,128)(2,1)S(1)} %collective-permute-done) | copy-start | bytes 48388
  30.3 4.5 %copy-start.3 = (bf16[256,2688]{1,0:T(8,128)(2,1)}, bf16[256,2688]{1,0:T(8,128)(2,1)S(1)}, u32[]{:S(2)}) copy-start(bf16[256,2688]{1,0:T(8,128)(2,1)S(1)} %get-tuple-element.32.x_ref) | copy-start | bytes 4128772
  108.9 7.4 %copy-start.13 = (f32[2688]{0:T(1024)S(1)}, f32[2688]{0:T(1024)}, u32[]{:S(2)}) copy-start(f32[2688]{0:T(1024)} %copy-done.12) | copy-start | bytes 32260
  108.9 7.4 %copy-start.15 = (f32[2688]{0:T(1024)S(1)}, f32[2688]{0:T(1024)}, u32[]{:S(2)}) copy-start(f32[2688]{0:T(1024)} %copy-done.14) | copy-start | bytes 32260
  108.9 7.4 %copy-start.17 = (f32[2688]{0:T(1024)S(1)}, f32[2688]{0:T(1024)}, u32[]{:S(2)}) copy-start(f32[2688]{0:T(1024)} %copy-done.16) | copy-start | bytes 32260
  108.9 7.4 %copy-start.19 = (f32[2688]{0:T(1024)S(1)}, f32[2688]{0:T(1024)}, u32[]{:S(2)}) copy-start(f32[2688]{0:T(1024)} %copy-done.18) | copy-start | bytes 32260
  124.6 44.9 %copy-start.6 = (bf16[259,2688]{1,0:T(8,128)(2,1)S(1)}, bf16[259,2688]{1,0:T(8,128)(2,1)}, u32[]{:S(2)}) copy-start(bf16[259,2688]{1,0:T(8,128)(2,1)} %add_convert_fusion) | copy-start | bytes 4177156
  163.0 6.5 %collective-permute-start.1 = (bf16[3,2688]{1,0:T(4,128)(2,1)S(1)}, bf16[3,2688]{1,0:T(4,128)(2,1)S(1)}, u32[]{:S(2)}, u32[]{:S(2)}) collective-permute-start(bf16[3,2688]{1,0:T(4,128)(2,1)S(1)} %add_convert_fusion.5), channel_id=1, source_target_pairs={{16,0},{32,16},{48,32},{64,48},{80,64},{96,80},{112,96},{128,112},... | collective-permute-start | bytes 48392 | tf_op jit(solution)/shard_map/ppermute | solution.py:23
  (20 other events, 41.0 us)

commit v3 on v2

--- a/solution.py
+++ b/solution.py
@@ -70,7 +70,7 @@
 
 def core_kernel(
     x_ref, dy_ref, steps_ref, docc_ref, docr_ref, skip_ref, parts_ref, decay_ref,
-    dx_ref, rows_ref, xdy_ref, dbc_ref, out_ref,
+    dx_ref, rows_ref, xdy_ref, dbc_ref, in_ref, adj_ref,
     scores, masked, gacc,
     other, theirs, comb, chain, got, chains, turned, result, lend, landed,
     pair_sems, send_a, recv_a, send_d, recv_d, send_b, recv_b,
@@ -202,18 +202,24 @@
     def _(k):
         back(k).wait()
 
+    def place(i, half, value):
+        lanes = pl.ds(pl.multiple_of(half * shape[1], shape[1]), shape[1])
+        in_ref[i * rows : (i + 1) * rows, lanes] = value[:rows]
+        adj_ref[i * rows : (i + 1) * rows, lanes] = value[rows:]
+
     for i in range(chips):
         value = result[i].astype(F32)
         here = jnp.where(keep_other, 1.0, yours_wide) * value
         here = here + jnp.where(keep_other, 0.0, other[i].astype(F32))
         there = jnp.where(keep_other, mine_wide, 1.0) * value
         there = there + jnp.where(keep_other, parts_ref[side, i].astype(F32), 0.0)
-        out_ref[side, i] = here.astype(BF16)
+        place(i, side, here)
         lend[i] = there.astype(BF16)
     lends = swap(lend, landed, 2)
     lends.start()
     lends.wait()
-    out_ref[1 - side] = landed[...]
+    for i in range(chips):
+        place(i, 1 - side, landed[i].astype(F32))
 
 
 def core(activated, dy, cum, step, docs, skip_wide, parts, decay):
@@ -227,16 +233,17 @@
     dma = pltpu.SemaphoreType.DMA
     half = pltpu.VMEM(parts.shape[1:], BF16)
     line = pltpu.VMEM((1, 128), F32)
-    dx, rows, xdy, dbc, carried = pl.pallas_call(
+    dx, rows, xdy, dbc, incoming, adjoint = pl.pallas_call(
         core_kernel,
         in_specs=[vmem] * 8,
-        out_specs=[vmem] * 5,
+        out_specs=[vmem] * 6,
         out_shape=[
             jax.ShapeDtypeStruct((length, DIN), BF16),
             jax.ShapeDtypeStruct((PAIRS, 4, length), F32),
             jax.ShapeDtypeStruct((PAIRS, 1, 2 * P_SIZE), F32),
             jax.ShapeDtypeStruct((length, 2 * N), F32),
-            jax.ShapeDtypeStruct(parts.shape, BF16),
+            jax.ShapeDtypeStruct((N, DIN), F32),
+            jax.ShapeDtypeStruct((N, DIN), F32),
         ],
         scratch_shapes=[
             *[pltpu.VMEM((length, length), F32)] * 3,
@@ -252,7 +259,113 @@
         jnp.pad(decay, (0, 128 - H))[None, :],
     )
     xdx, col = rows[:, :2].reshape(H, length), rows[:, 2:].reshape(H, length)
-    return dx, xdx, col, xdy, dbc, carried
+    return dx, xdx, col, xdy, dbc, incoming, adjoint
+
+
+def finish_kernel(
+    bc_ref, pre_ref, own_ref, rim_ref, taps_ref, keep_ref, tail_ref, weighted_ref, led_ref,
+    dx_ref, dbc_ref, in_ref, adj_ref,
+    out_ref, edge_ref, grads_ref, lines_ref, met_ref,
+    ext, terms, acc,
+):
+    j = pl.program_id(0)
+    length, wide = own_ref.shape
+    b, c = bc_ref[:, :N], bc_ref[:, N:]
+
+    def convolve(grad_act):
+        grad_act = grad_act.astype(BF16).astype(F32)
+        pre = pre_ref[...]
+        gate = jax.nn.sigmoid(pre)
+        grad_pre = grad_act * (gate * (1.0 + pre * (1.0 - gate)))
+        ext[:8] = rim_ref[...]
+        ext[8:] = own_ref[...].astype(F32)
+        body, edge = None, None
+        for k in range(4):
+            kept = grad_pre * keep_ref[:, k : k + 1]
+            grads_ref[k : k + 1, :] = jnp.sum(
+                kept * ext[5 + k : 5 + k + length, :], axis=0, keepdims=True
+            )
+            terms[k, 8 : 8 + length] = kept * taps_ref[k : k + 1, :]
+            here = terms[k, 11 - k : 11 - k + length, :]
+            front = terms[k, 8 - k : 16 - k, :]
+            body = here if body is None else body + here
+            edge = front if edge is None else edge + front
+        grads_ref[4:5, :] = jnp.sum(grad_pre, axis=0, keepdims=True)
+        grads_ref[5:8, :] = jnp.zeros((3, wide), F32)
+        out_ref[...] = body.astype(BF16)
+        edge_ref[...] = edge.astype(BF16)
+
+    @pl.when(j == 0)
+    def _():
+        terms[...] = jnp.zeros_like(terms)
+        acc[...] = dbc_ref[...]
+
+    @pl.when(j < PAIRS)
+    def _():
+        weighted, led = weighted_ref[...], led_ref[...]
+        incoming, adjoint = in_ref[...], adj_ref[...]
+        met_ref[0] = jnp.sum(incoming * adjoint, axis=0, keepdims=True)
+        incoming, adjoint = incoming.astype(BF16), adjoint.astype(BF16)
+        outer = dot(c, incoming, 1, 0)
+        spread = dot(b, adjoint, 1, 0)
+        acc[:, :N] += dot(weighted, adjoint, 1, 1)
+        acc[:, N:] += dot(led, incoming, 1, 1)
+        head = lax.broadcasted_iota(jnp.int32, (8, wide), 0)
+        pick = lax.broadcasted_iota(jnp.int32, (8, wide), 1) // P_SIZE == head
+        pick = jnp.where(pick, 1.0, 0.0).astype(BF16)
+        values = (led.astype(F32) * outer, spread * weighted.astype(F32))
+        for i, value in enumerate(values):
+            high = value.astype(BF16)
+            low = (value - high.astype(F32)).astype(BF16)
+            line = dot(pick, high, 1, 1) + dot(pick, low, 1, 1)
+            lines_ref[0, 2 * i : 2 * i + 2, :] = line[:2]
+        convolve(dx_ref[...].astype(F32) + spread * tail_ref[...])
+
+    @pl.when(j == PAIRS)
+    def _():
+        convolve(acc[...])
+
+
+def finish(
+    activated, pre, own_rows, rim_rows, conv_weight, keeps, tail_wide, weighted, led,
+    dx, dbc, incoming, adjoint,
+):
+    length, channels = own_rows.shape
+    taps = conv_weight.shape[0]
+    wide = 2 * P_SIZE
+    every = lambda rows: pl.BlockSpec((rows, wide), lambda j: (0, j))
+    inner = lambda rows: pl.BlockSpec((rows, wide), lambda j: (0, jnp.minimum(j, PAIRS - 1)))
+    lines = lambda rows, lanes: pl.BlockSpec(
+        (1, rows, lanes), lambda j: (jnp.minimum(j, PAIRS - 1), 0, 0)
+    )
+    fixed = lambda rows, lanes, at: pl.BlockSpec((rows, lanes), lambda j: (0, at))
+    return pl.pallas_call(
+        finish_kernel,
+        grid=(PAIRS + 1,),
+        in_specs=[
+            fixed(length, wide, PAIRS), every(length), every(length), every(8), every(taps),
+            fixed(length, taps, 0), inner(length), inner(length), inner(length),
+            inner(length), fixed(length, wide, 0), inner(N), inner(N),
+        ],
+        out_specs=[every(length), every(8), every(8), lines(4, length), lines(1, wide)],
+        out_shape=[
+            jax.ShapeDtypeStruct((length, channels), BF16),
+            jax.ShapeDtypeStruct((8, channels), BF16),
+            jax.ShapeDtypeStruct((8, channels), F32),
+            jax.ShapeDtypeStruct((PAIRS, 4, length), F32),
+            jax.ShapeDtypeStruct((PAIRS, 1, wide), F32),
+        ],
+        scratch_shapes=[
+            pltpu.VMEM((8 + length, wide), F32),
+            pltpu.VMEM((taps, 16 + length, wide), F32),
+            pltpu.VMEM((length, wide), F32),
+        ],
+        name="finish",
+    )(
+        activated, pre, own_rows, jnp.pad(rim_rows.astype(F32), ((9 - taps, 0), (0, 0))),
+        conv_weight, jnp.concatenate(keeps, axis=1).astype(F32), tail_wide, weighted, led,
+        dx, dbc, incoming, adjoint,
+    )
 
 
 def total_kernel(
@@ -374,7 +487,6 @@
         return high.astype(BF16), (v - high).astype(BF16)
 
     widen = lambda v: dot(jnp.concatenate(halves(v)), twice, 0, 0)
-    narrow = lambda v: sum(dot(expand, part, 1, 1) for part in halves(v))
     upto = jnp.triu(jnp.ones((length, length), F32))
 
     offset = lax.axis_index("ctx") * length
@@ -413,23 +525,17 @@
     rows = N // chips
     split = lambda v: v.astype(BF16).reshape(chips, rows, 2, DIN // 2).transpose(2, 0, 1, 3)
     parts = jnp.concatenate([split(local), split(seeded)], axis=2)
-    dx, xdx, col, xdy, dbc, carried = core(
+    dx, xdx, col, xdy, dbc, incoming, adjoint = core(
         activated, dy, cum, step, docs, jnp.repeat(d_skip, P_SIZE), parts, decay
     )
-    join = lambda v: v.transpose(1, 2, 0, 3).reshape(N, DIN)
-    incoming, adjoint = join(carried[:, :, :rows]), join(carried[:, :, rows:])
-
-    outer = dot(c, incoming, 1, 0)
-    spread = dot(b, adjoint, 1, 0)
-    from_lead = narrow(led.astype(F32) * outer)
-    from_tail = narrow(spread * weighted.astype(F32))
-    db = dbc[:, :N] + dot(weighted, adjoint, 1, 1)
-    dc = dbc[:, N:] + dot(led, incoming, 1, 1)
-    grad_act = jnp.concatenate([dx.astype(F32) + spread * tail_wide, db, dc], axis=1)
-    grad_act = grad_act.astype(BF16).astype(F32)
-
-    met = jnp.sum(adjoint.astype(F32) * incoming.astype(F32), axis=0, keepdims=True)
-    grad_last = jnp.sum(from_tail, axis=1, keepdims=True) + narrow(met) * decay[:, None]
+    own_grad, edge, grad_taps, lines, met = finish(
+        activated, pre, own_rows, rim_rows, conv_weight, keeps, tail_wide, weighted, led,
+        dx, dbc, incoming, adjoint,
+    )
+    from_lead = lines[:, :2].reshape(H, length)
+    from_tail = lines[:, 2:].reshape(H, length)
+    met = jnp.sum(met.reshape(H, P_SIZE), axis=1, keepdims=True)
+    grad_last = jnp.sum(from_tail, axis=1, keepdims=True) + met * decay[:, None]
     grad_cum = col - xdx + from_lead - from_tail
     grad_scaled = dot(grad_cum, upto, 1, 1, HIGHEST) + grad_last
     grad_step = (xdx + from_tail) / step + grad_scaled * rate
@@ -439,23 +545,15 @@
     grad_dtb = jnp.sum(grad_raw, axis=1)
     grad_skip = jnp.sum(xdy.reshape(H, P_SIZE), axis=1)
 
-    gate = jax.nn.sigmoid(pre)
-    grad_pre = grad_act * (gate * (1.0 + pre * (1.0 - gate)))
-    grad_weight = jnp.stack([jnp.sum(grad_pre * shifted[k], axis=0) for k in range(taps)])
-    grad_bias = jnp.sum(grad_pre, axis=0)
-    grad_ext = 0.0
-    for k in range(taps):
-        term = jnp.where(keeps[k], conv_weight[k][None, :] * grad_pre, 0.0)
-        grad_ext = grad_ext + jnp.pad(term, ((k, taps - 1 - k), (0, 0)))
-    grad_ext = grad_ext.astype(BF16)
-    returned = from_behind(grad_ext[: taps - 1], "ctx", -1).astype(F32)
-    own_grad = grad_ext[taps - 1 :].astype(F32)
-    own_grad = own_grad + jnp.pad(returned, ((length - taps + 1, 0), (0, 0)))
+    grad_weight, grad_bias = grad_taps[:taps], grad_taps[taps]
+    returned = from_behind(edge[: taps - 1], "ctx", -1).astype(F32)
+    last = own_grad[length - 8 :].astype(F32) + jnp.pad(returned, ((9 - taps, 0), (0, 0)))
+    own_grad = lax.dynamic_update_slice(own_grad, last.astype(BF16), (length - 8, 0))
     mine = (grad_weight, grad_bias, grad_dtb, grad_alog, grad_skip)
     total = total_sum(jnp.concatenate([part.reshape(-1) for part in mine]))
     ends = np.cumsum([part.size for part in mine])[:-1].tolist()
     sums = [part.reshape(like.shape) for part, like in zip(jnp.split(total, ends), mine)]
-    return (own_grad.astype(BF16)[None], grad_raw16[None], *sums)
+    return (own_grad[None], grad_raw16[None], *sums)
 
 
 def solution(mesh):

time: 172 us -> 168 us (0.977)
  Pallas kernels: 90.9 us -> 114 us
  other arithmetic: 29.2 us -> 16.5 us
  matrix products: 22.2 us -> 11.3 us
  local copies, waits for them, and re-layouts: 18.6 us -> 15.6 us
    pallas_call x1 -> x2, Pallas kernels: 55.2 us -> 74.1 us  [the longest x1 55.3 us: core(): pl.pallas_call(core_kernel, in_specs=[vmem] * 8, out_specs=[vmem] * 6, ou...]
    dot_general x18 -> x8, matrix products: 22.2 us -> 11.3 us  [dot(): lax.dot_general(a, b, (((ca,), (cb,)), ((), ())), precision=precision, pr...]
    reduce_sum x2, other arithmetic: 8.93 us -> 1.18 us  [the longest x1 1.07 us: per_device(): grad_last = jnp.sum(from_tail, axis=1, keepdims=True) + met * decay[:, None]]
    pallas_call x1, Pallas kernels: 35.8 us -> 39.8 us  [total_sum(): pl.pallas_call(total_kernel, out_shape=jax.ShapeDtypeStruct(padded.shape,...]
    concatenate x1, local copies, waits for them, and re-layouts: 3.3 us -> 0.08 us  [finish(): jnp.concatenate(keeps, axis=1).astype(F32)]
    slice x2 -> x5, local copies, waits for them, and re-layouts: 1.65 us -> 4.36 us  [the longest x2 1.93 us: per_device(): grad_weight, grad_bias = (grad_taps[:taps], grad_taps[taps])]
    transpose x3 -> x0, local copies, waits for them, and re-layouts: 2.22 us -> none  [per_device(): join = lambda v: v.transpose(1, 2, 0, 3).reshape(N, DIN)]
    convert_element_type x3 -> x2, other arithmetic: 3.36 us -> 1.44 us  [the longest x1 1.37 us: per_device(): lead = jnp.exp(cum) * (docs == prev_doc).astype(F32)[None, :]]
  transfers between devices with their start and end apart: 2 -> 2, of which waited for: 0 -> 0; matrix products, arithmetic and copies ran while one was open for 11% -> 14% of each run, Pallas kernels for 0% -> 24%
where the time goes in v3:
time: 168 us; the launch traced here: 167 us
  Pallas kernels  114 us (68%)
  other arithmetic  16.5 us (10%)
  local copies, waits for them, and re-layouts  15.6 us (9%)
  matrix products  11.3 us (7%)
  starting transfers between devices  6.98 us (4%)
  between operations  2.47 us (1%)
    pallas_call x1, Pallas kernels, core(): pl.pallas_call(core_kernel, in_specs=[vmem] * 8, out_specs=[vmem] * 6, ou...  55.3 us
    pallas_call x1, Pallas kernels, total_sum(): pl.pallas_call(total_kernel, out_shape=jax.ShapeDtypeStruct(padded.shape,...  39.8 us
    pallas_call x1, Pallas kernels, finish(): pl.pallas_call(finish_kernel, grid=(PAIRS + 1,), in_specs=[fixed(length,...  18.8 us
    dot_general x8, matrix products, dot(): lax.dot_general(a, b, (((ca,), (cb,)), ((), ())), precision=precision, pr...  11.3 us
    convert_element_type x1, other arithmetic, per_device(): activated = jax.nn.silu(pre).astype(BF16)  7.2 us
    ppermute x2, starting transfers between devices, from_behind(): lax.ppermute(value, axis, [(source, source + steps) for source in range(l...  6.98 us
    split x3, local copies, waits for them, and re-layouts, per_device(): jnp.split(total, ends)  3.49 us
  transfers between devices with their start and end apart: 2, of which 0 were waited for; matrix products, arithmetic and copies ran while one was open for 14% of the time, Pallas kernels for 24%

profile of v3, /device:TPU:1, one launch (start us, length us, event | category | flops | bytes accessed | tf_op | source)
XLA Modules:
  0.0 166.8 jit_solution(8430336463633226951)
XLA Ops:
  0.7 0.9 slice_bitcast_fusion
  1.5 4.9 %collective-permute-start = (bf16[3,2688]{1,0:T(4,128)(2,1)S(1)}, bf16[3,2688]{1,0:T(4,128)(2,1)S(1)}, u32[]{:S(2)}, u32[]{:S(2)}) collective-permute-start(bf16[3,2688]{1,0:T(4,128)(2,1)S(1)} %slice_bitcast_fusion), channel_id=1, source_target_pairs={{0,16},{16,32},{32,48},{48,64},{64,80},{80,96},{96,112},{112,128},... | collective-permute-start | bytes 48392 | tf_op jit(solution)/shard_map/ppermute | solution.py:23
  6.5 0.8 reduce-window_clone.1
  10.0 1.4 compare_convert_fusion
  12.0 1.1 fusion.5
  13.2 0.8 compare_select_fusion
  14.2 1.1 slice_reduce_fusion.4
  15.4 1.6 fusion.38
  17.1 2.1 %fusion.37 = f32[256,2560]{1,0:T(8,128)} fusion(bf16[40,2560]{1,0:T(8,128)(2,1)S(1)} %copy-done.4, f32[40,256]{1,0:T(8,128)S(1)} %fusion.5, f32[256]{0:T(256)S(1)} %get-tuple-element.47, f32[40]{0:T(128)S(1)} %bitcast.121, bf16[1,256,40]{1,2,0:T(8,128)(2,1)S(1)} %copy-done.8, f32[40]{0:T(128)S(1)} %copy-done.18), kind=kOutput, calls=%fused_computation.63 | convolution fusion | flops 52561920 | bytes 2889024 | tf_op jit(solution)/shard_map/dot_general | solution.py:33
  19.8 0.9 maximum_maximum_fusion.steps_ref
  23.8 7.2 %multiply_convert_fusion = (bf16[256,2688]{1,0:T(8,128)(2,1)S(1)}, f32[256,2688]{1,0:T(8,128)}) fusion(bf16[256,2688]{1,0:T(8,128)(2,1)} %bitcast.112, f32[2688]{0:T(1024)S(1)} %get-tuple-element.32, bf16[3,2688]{1,0:T(4,128)(2,1)S(1)} %collective-permute-done, pred[256]{0:T(512)(128)(4,1)S(1)} %get-tuple-element.48, f32[2688]{0:T(1024)S(1)} %get-tuple-element.30, ...), kind=kLoop, calls=%fused_computation.6 | loop fusion | flops 19955712 | bytes 5575680 | tf_op jit(solution)/shard_map/convert_element_type | solution.py:506
  31.5 4.0 %multiply_convert_fusion.1 = (bf16[256,2560]{1,0:T(8,128)(2,1)S(1)}, f32[256,2560]{1,0:T(8,128)}) fusion(bf16[256,2688]{1,0:T(8,128)(2,1)S(1)} %get-tuple-element.35.x_ref.bc_ref, f32[256,2560]{1,0:T(8,128)} %fusion.37, bf16[40,2560]{1,0:T(8,128)(2,1)S(1)} %copy-done.4, f32[256]{0:T(256)S(1)} %get-tuple-element.47, f32[40,256]{1,0:T(8,128)} %copy-done.7, ...), kind=kOutput, calls=%fused_computation.8 | convolution fusion | flops 55193600 | bytes 8131904 | tf_op jit(solution)/shard_map/dot_general | solution.py:33
  36.3 1.2 pad_maximum_fusion.1.parts_ref
  37.5 55.3 %core.1 = (bf16[256,2560]{1,0:T(8,128)(2,1)}, f32[20,4,256]{2,1,0:T(4,128)}, f32[20,1,128]{2,1,0:T(1,128)}, f32[256,128]{1,0:T(8,128)}, f32[64,2560]{1,0:T(8,128)}, /*index=5*/f32[64,2560]{1,0:T(8,128)}) custom-call(bf16[256,2688]{1,0:T(8,128)(2,1)} %copy-done, bf16[256,2560]{1,0:T(8,128)(2,1)} %bitcast.114, f32[20,8,256]{2,1,0:T(8,128)} %maximum_maximum_fusion.steps_ref, ...), custom_call_target="tpu_custom_call" | custom-call | tf_op jit(solution)/shard_map/core/pallas_call | solution.py:236
  93.5 18.8 %finish.1 = (bf16[256,2688]{1,0:T(8,128)(2,1)}, bf16[8,2688]{1,0:T(8,128)(2,1)}, f32[8,2688]{1,0:T(8,128)}, f32[20,4,256]{2,1,0:T(4,128)}, f32[20,1,128]{2,1,0:T(1,128)}) custom-call(bf16[256,2688]{1,0:T(8,128)(2,1)} %copy-done, f32[256,2688]{1,0:T(8,128)} %get-tuple-element.36.pre_ref, bf16[256,2688]{1,0:T(8,128)(2,1)} %bitcast.113, ...), custom_call_target="tpu_custom_call" | custom-call | tf_op jit(solution)/shard_map/finish/pallas_call | solution.py:342
  112.3 1.0 slice_reduce_fusion
  113.4 0.9 slice.117
  116.2 2.0 %collective-permute-start.1 = (bf16[3,2688]{1,0:T(4,128)(2,1)S(1)}, bf16[3,2688]{1,0:T(4,128)(2,1)S(1)}, u32[]{:S(2)}, u32[]{:S(2)}) collective-permute-start(bf16[3,2688]{1,0:T(4,128)(2,1)S(1)} %slice.112), channel_id=1, source_target_pairs={{16,0},{32,16},{48,32},{64,48},{80,64},{96,80},{112,96},{128,112},... | collective-permute-start | bytes 48392 | tf_op jit(solution)/shard_map/ppermute | solution.py:23
  118.4 1.1 slice_reduce_fusion.5
  119.7 1.2 fusion.49
  121.6 39.8 %total.1 = f32[32,4,128]{2,1,0:T(4,128)} custom-call(f32[32,4,128]{2,1,0:T(4,128)} %bitcast.116), custom_call_target="tpu_custom_call" | custom-call | tf_op jit(solution)/shard_map/total/pallas_call | solution.py:457
  161.4 1.4 fusion.52
  162.8 1.3 split.20
  165.7 1.1 copy-done.6
  (108 shorter events, 12.5 us)
Async XLA Ops:
  0.6 16.4 %copy-start.4 = (bf16[40,2560]{1,0:T(8,128)(2,1)S(1)}, bf16[40,2560]{1,0:T(8,128)(2,1)}, u32[]{:S(2)}) copy-start(bf16[40,2560]{1,0:T(8,128)(2,1)} %constant.57) | copy-start | bytes 614404
  0.6 16.4 %copy-start.18 = (f32[40]{0:T(128)S(1)}, f32[40]{0:T(128)}, u32[]{:S(2)}) copy-start(f32[40]{0:T(128)} %param.14) | copy-start | bytes 484
  0.7 16.4 %copy-start.8 = (bf16[1,256,40]{1,2,0:T(8,128)(2,1)S(1)}, bf16[1,256,40]{1,2,0:T(8,128)(2,1)}, u32[]{:S(2)}) copy-start(bf16[1,256,40]{1,2,0:T(8,128)(2,1)} %param.11) | copy-start | bytes 61444
  1.5 22.2 %collective-permute-start = (bf16[3,2688]{1,0:T(4,128)(2,1)S(1)}, bf16[3,2688]{1,0:T(4,128)(2,1)S(1)}, u32[]{:S(2)}, u32[]{:S(2)}) collective-permute-start(bf16[3,2688]{1,0:T(4,128)(2,1)S(1)} %slice_bitcast_fusion), channel_id=1, source_target_pairs={{0,16},{16,32},{32,48},{48,64},{64,80},{80,96},{96,112},{112,128},... | collective-permute-start | bytes 48392 | tf_op jit(solution)/shard_map/ppermute | solution.py:23
  6.5 7.7 %copy-start.22 = (s32[256]{0:T(256)}, s32[256]{0:T(256)S(1)}, u32[]{:S(2)}) copy-start(s32[256]{0:T(256)S(1)} %iota_add_fusion) | copy-start | bytes 3076
  13.1 6.1 %copy-start.7 = (f32[40,256]{1,0:T(8,128)}, f32[40,256]{1,0:T(8,128)S(1)}, u32[]{:S(2)}) copy-start(f32[40,256]{1,0:T(8,128)S(1)} %fusion.5) | copy-start | bytes 122884
  15.4 3.8 %copy-start.3 = (bf16[1,256,2560]{2,1,0:T(8,128)(2,1)S(1)}, bf16[1,256,2560]{2,1,0:T(8,128)(2,1)}, u32[]{:S(2)}) copy-start(bf16[1,256,2560]{2,1,0:T(8,128)(2,1)} %param.17) | copy-start | bytes 3932164
  19.2 4.6 %copy-start.13 = (f32[2688]{0:T(1024)S(1)}, f32[2688]{0:T(1024)}, u32[]{:S(2)}) copy-start(f32[2688]{0:T(1024)} %param.13) | copy-start | bytes 32260
  19.8 11.2 %copy-start.2 = (bf16[256,2560]{1,0:T(8,128)(2,1)}, bf16[256,2560]{1,0:T(8,128)(2,1)S(1)}, u32[]{:S(2)}) copy-start(bf16[256,2560]{1,0:T(8,128)(2,1)S(1)} %fusion.1.led_ref) | copy-start | bytes 3932164
  21.3 9.7 %copy-start.15 = (s32[256]{0:T(256)}, s32[256]{0:T(256)S(1)}, u32[]{:S(2)}) copy-start(s32[256]{0:T(256)S(1)} %slice.94) | copy-start | bytes 3076
  23.8 7.2 %copy-start.10 = (bf16[3,2688]{1,0:T(4,128)(2,1)}, bf16[3,2688]{1,0:T(4,128)(2,1)S(1)}, u32[]{:S(2)}) copy-start(bf16[3,2688]{1,0:T(4,128)(2,1)S(1)} %collective-permute-done) | copy-start | bytes 48388
  31.0 4.6 %copy-start = (bf16[256,2688]{1,0:T(8,128)(2,1)}, bf16[256,2688]{1,0:T(8,128)(2,1)S(1)}, u32[]{:S(2)}) copy-start(bf16[256,2688]{1,0:T(8,128)(2,1)S(1)} %get-tuple-element.35.x_ref.bc_ref) | copy-start | bytes 4128772
  35.5 57.2 %copy-start.1 = (bf16[256,2560]{1,0:T(8,128)(2,1)}, bf16[256,2560]{1,0:T(8,128)(2,1)S(1)}, u32[]{:S(2)}) copy-start(bf16[256,2560]{1,0:T(8,128)(2,1)S(1)} %get-tuple-element.53.weighted_ref) | copy-start | bytes 3932164
  36.3 56.5 %copy-start.11 = (bf16[3,2688]{1,0:T(4,128)(2,1)S(1)}, bf16[3,2688]{1,0:T(4,128)(2,1)}, u32[]{:S(2)}) copy-start(bf16[3,2688]{1,0:T(4,128)(2,1)} %copy-done.10) | copy-start | bytes 48388
  93.4 22.3 %copy-start.14 = (f32[20,1,128]{2,1,0:T(1,128)S(1)}, f32[20,1,128]{2,1,0:T(1,128)}, u32[]{:S(2)}) copy-start(f32[20,1,128]{2,1,0:T(1,128)} %get-tuple-element.28) | copy-start | bytes 30724
  93.4 24.8 %copy-start.12 = (f32[20,4,256]{2,1,0:T(4,128)S(1)}, f32[20,4,256]{2,1,0:T(4,128)}, u32[]{:S(2)}) copy-start(f32[20,4,256]{2,1,0:T(4,128)} %get-tuple-element.24) | copy-start | bytes 245764
  93.5 26.2 %copy-start.17 = (f32[40,1]{0,1:T(1,128)S(1)}, f32[40,1]{0,1:T(1,128)}, u32[]{:S(2)}) copy-start(f32[40,1]{0,1:T(1,128)} %copy-done.16) | copy-start | bytes 484
  93.5 26.2 %copy-start.9 = (bf16[1,256,40]{1,2,0:T(8,128)(2,1)S(1)}, bf16[1,256,40]{1,2,0:T(8,128)(2,1)}, u32[]{:S(2)}) copy-start(bf16[1,256,40]{1,2,0:T(8,128)(2,1)} %param.11) | copy-start | bytes 61444
  93.5 26.2 %copy-start.19 = (f32[40]{0:T(128)S(1)}, f32[40]{0:T(128)}, u32[]{:S(2)}) copy-start(f32[40]{0:T(128)} %param.14) | copy-start | bytes 484
  93.5 26.2 %copy-start.23 = (s32[256]{0:T(256)S(1)}, s32[256]{0:T(256)}, u32[]{:S(2)}) copy-start(s32[256]{0:T(256)} %copy-done.22) | copy-start | bytes 3076
  93.5 26.2 %copy-start.25 = (f32[40]{0:T(128)S(1)}, f32[40]{0:T(128)}, u32[]{:S(2)}) copy-start(f32[40]{0:T(128)} %copy-done.24) | copy-start | bytes 484
  93.5 27.4 %copy-start.21 = (f32[40]{0:T(128)S(1)}, f32[40]{0:T(128)}, u32[]{:S(2)}) copy-start(f32[40]{0:T(128)} %param.15) | copy-start | bytes 484
  112.3 53.3 %copy-start.5 = (bf16[256,2688]{1,0:T(8,128)(2,1)S(1)}, bf16[256,2688]{1,0:T(8,128)(2,1)}, u32[]{:S(2)}) copy-start(bf16[256,2688]{1,0:T(8,128)(2,1)} %get-tuple-element.22) | copy-start | bytes 4128772
  116.2 49.5 %collective-permute-start.1 = (bf16[3,2688]{1,0:T(4,128)(2,1)S(1)}, bf16[3,2688]{1,0:T(4,128)(2,1)S(1)}, u32[]{:S(2)}, u32[]{:S(2)}) collective-permute-start(bf16[3,2688]{1,0:T(4,128)(2,1)S(1)} %slice.112), channel_id=1, source_target_pairs={{16,0},{32,16},{48,32},{64,48},{80,64},{96,80},{112,96},{128,112},... | collective-permute-start | bytes 48392 | tf_op jit(solution)/shard_map/ppermute | solution.py:23
  (4 other events, 8.2 us)

commit v4 on v3

--- a/solution.py
+++ b/solution.py
@@ -369,7 +369,7 @@
 
 
 def total_kernel(
-    v_ref, out_ref, got, mid, across, last, spread,
+    wide_ref, small_ref, wide_out, small_out, v_ref, got, mid, across, last, spread,
     send_a, recv_a, send_b, recv_b, send_c, recv_c,
 ):
     nc, nb = lax.axis_size("ctx"), lax.axis_size("bal")
@@ -387,6 +387,12 @@
             device_id={axis: peer}, device_id_type=pl.DeviceIdType.MESH,
         )
 
+    blocks = wide_ref.shape[1] // 128
+    for i in range(blocks):
+        v_ref[i] = wide_ref[:, i * 128 : (i + 1) * 128]
+    v_ref[blocks] = small_ref[...]
+    v_ref[blocks + 1 :] = jnp.zeros((nc - blocks - 1, *small_ref.shape), F32)
+
     barrier = pltpu.get_barrier_semaphore()
 
     @pl.loop(1, nc)
@@ -446,31 +452,33 @@
     def _(k):
         third(k).wait()
 
-    out_ref[...] = spread[...]
-
-
-def total_sum(vector):
+    for i in range(blocks):
+        wide_out[:, i * 128 : (i + 1) * 128] = spread[i]
+    small_out[...] = spread[blocks]
+
+
+def total_sum(wide, small):
     nc, nb = lax.axis_size("ctx"), lax.axis_size("bal")
-    rows = -(-vector.shape[0] // (nc * 128))
-    padded = jnp.pad(vector, (0, nc * rows * 128 - vector.shape[0])).reshape(nc, rows, 128)
+    piece = small.shape
+    vmem = pl.BlockSpec(memory_space=pltpu.VMEM)
     dma = pltpu.SemaphoreType.DMA
-    summed = pl.pallas_call(
+    return pl.pallas_call(
         total_kernel,
-        out_shape=jax.ShapeDtypeStruct(padded.shape, F32),
-        in_specs=[pl.BlockSpec(memory_space=pltpu.VMEM)],
-        out_specs=pl.BlockSpec(memory_space=pltpu.VMEM),
+        out_shape=[jax.ShapeDtypeStruct(wide.shape, F32), jax.ShapeDtypeStruct(piece, F32)],
+        in_specs=[vmem] * 2,
+        out_specs=[vmem] * 2,
         scratch_shapes=[
-            pltpu.VMEM((nc, rows, 128), F32),
-            pltpu.VMEM((rows, 128), F32),
-            pltpu.VMEM((nb, rows, 128), F32),
-            pltpu.VMEM((rows, 128), F32),
-            pltpu.VMEM((nc, rows, 128), F32),
+            pltpu.VMEM((nc, *piece), F32),
+            pltpu.VMEM((nc, *piece), F32),
+            pltpu.VMEM(piece, F32),
+            pltpu.VMEM((nb, *piece), F32),
+            pltpu.VMEM(piece, F32),
+            pltpu.VMEM((nc, *piece), F32),
             dma((nc,)), dma((nc,)), dma((nb,)), dma((nb,)), dma((nc,)), dma((nc,)),
         ],
         compiler_params=pltpu.CompilerParams(collective_id=0, has_side_effects=True),
         name="total",
-    )(padded)
-    return summed.reshape(-1)[: vector.shape[0]]
+    )(wide, small)
 
 
 def per_device(xbc, dt_raw, conv_weight, conv_bias, dt_bias, a_log, d_skip, grad_out, doc_lengths):
@@ -545,14 +553,12 @@
     grad_dtb = jnp.sum(grad_raw, axis=1)
     grad_skip = jnp.sum(xdy.reshape(H, P_SIZE), axis=1)
 
-    grad_weight, grad_bias = grad_taps[:taps], grad_taps[taps]
     returned = from_behind(edge[: taps - 1], "ctx", -1).astype(F32)
     last = own_grad[length - 8 :].astype(F32) + jnp.pad(returned, ((9 - taps, 0), (0, 0)))
     own_grad = lax.dynamic_update_slice(own_grad, last.astype(BF16), (length - 8, 0))
-    mine = (grad_weight, grad_bias, grad_dtb, grad_alog, grad_skip)
-    total = total_sum(jnp.concatenate([part.reshape(-1) for part in mine]))
-    ends = np.cumsum([part.size for part in mine])[:-1].tolist()
-    sums = [part.reshape(like.shape) for part, like in zip(jnp.split(total, ends), mine)]
+    small = jnp.pad(jnp.stack([grad_dtb, grad_alog, grad_skip]), ((0, 5), (0, 128 - H)))
+    wide, small = total_sum(grad_taps, small)
+    sums = (wide[:taps], wide[taps], small[0, :H], small[1, :H], small[2, :H])
     return (own_grad[None], grad_raw16[None], *sums)
 
 

time: 168 us -> 172 us (1.024)
  Pallas kernels: 114 us -> 120 us
  local copies, waits for them, and re-layouts: 15.6 us -> 13.2 us
    pallas_call x1, Pallas kernels: 39.8 us -> 45.4 us  [total_sum(): pl.pallas_call(total_kernel, out_shape=[jax.ShapeDtypeStruct(wide.shape,...]
    split x3 -> x0, local copies, waits for them, and re-layouts: 3.49 us -> none  [per_device(): jnp.split(total, ends)]
  transfers between devices with their start and end apart: 2 -> 2, of which waited for: 0 -> 0; matrix products, arithmetic and copies ran while one was open for 14% -> 14% of each run, Pallas kernels for 24% -> 27%
where the time goes in v4:
time: 172 us; the launch traced here: 171 us
  Pallas kernels  120 us (70%)
  other arithmetic  17.1 us (10%)
  local copies, waits for them, and re-layouts  13.2 us (8%)
  matrix products  11.3 us (7%)
  starting transfers between devices  6.99 us (4%)
  between operations  2.46 us (1%)
    pallas_call x1, Pallas kernels, core(): pl.pallas_call(core_kernel, in_specs=[vmem] * 8, out_specs=[vmem] * 6, ou...  55.3 us
    pallas_call x1, Pallas kernels, total_sum(): pl.pallas_call(total_kernel, out_shape=[jax.ShapeDtypeStruct(wide.shape,...  45.4 us
    pallas_call x1, Pallas kernels, finish(): pl.pallas_call(finish_kernel, grid=(PAIRS + 1,), in_specs=[fixed(length,...  18.8 us
    dot_general x8, matrix products, dot(): lax.dot_general(a, b, (((ca,), (cb,)), ((), ())), precision=precision, pr...  11.3 us
    convert_element_type x1, other arithmetic, per_device(): activated = jax.nn.silu(pre).astype(BF16)  7.2 us
    ppermute x2, starting transfers between devices, from_behind(): lax.ppermute(value, axis, [(source, source + steps) for source in range(l...  6.99 us
  transfers between devices with their start and end apart: 2, of which 0 were waited for; matrix products, arithmetic and copies ran while one was open for 14% of the time, Pallas kernels for 27%

profile of v4, /device:TPU:1, one launch (start us, length us, event | category | flops | bytes accessed | tf_op | source)
XLA Modules:
  0.0 170.7 jit_solution(10276331662184209299)
XLA Ops:
  0.7 0.9 slice_bitcast_fusion
  1.5 4.9 %collective-permute-start = (bf16[3,2688]{1,0:T(4,128)(2,1)S(1)}, bf16[3,2688]{1,0:T(4,128)(2,1)S(1)}, u32[]{:S(2)}, u32[]{:S(2)}) collective-permute-start(bf16[3,2688]{1,0:T(4,128)(2,1)S(1)} %slice_bitcast_fusion), channel_id=1, source_target_pairs={{0,16},{16,32},{32,48},{48,64},{64,80},{80,96},{96,112},{112,128},... | collective-permute-start | bytes 48392 | tf_op jit(solution)/shard_map/ppermute | solution.py:23
  6.5 0.8 reduce-window_clone.1
  10.0 1.4 compare_convert_fusion
  12.0 1.1 fusion.5
  13.2 0.8 compare_select_fusion
  14.2 1.1 slice_reduce_fusion.4
  15.4 1.6 fusion.38
  17.1 2.1 %fusion.37 = f32[256,2560]{1,0:T(8,128)} fusion(bf16[40,2560]{1,0:T(8,128)(2,1)S(1)} %copy-done.4, f32[40,256]{1,0:T(8,128)S(1)} %fusion.5, f32[256]{0:T(256)S(1)} %get-tuple-element.51, f32[40]{0:T(128)S(1)} %bitcast.126, bf16[1,256,40]{1,2,0:T(8,128)(2,1)S(1)} %copy-done.8, f32[40]{0:T(128)S(1)} %copy-done.18), kind=kOutput, calls=%fused_computation.63 | convolution fusion | flops 52561920 | bytes 2889024 | tf_op jit(solution)/shard_map/dot_general | solution.py:33
  19.8 0.9 maximum_maximum_fusion.steps_ref
  23.8 7.2 %multiply_convert_fusion = (bf16[256,2688]{1,0:T(8,128)(2,1)S(1)}, f32[256,2688]{1,0:T(8,128)}) fusion(bf16[256,2688]{1,0:T(8,128)(2,1)} %bitcast.120, f32[2688]{0:T(1024)S(1)} %get-tuple-element.36, bf16[3,2688]{1,0:T(4,128)(2,1)S(1)} %collective-permute-done, pred[256]{0:T(512)(128)(4,1)S(1)} %get-tuple-element.52, f32[2688]{0:T(1024)S(1)} %get-tuple-element.34, ...), kind=kLoop, calls=%fused_computation.6 | loop fusion | flops 19955712 | bytes 5575680 | tf_op jit(solution)/shard_map/convert_element_type | solution.py:514
  31.5 4.0 %multiply_convert_fusion.1 = (bf16[256,2560]{1,0:T(8,128)(2,1)S(1)}, f32[256,2560]{1,0:T(8,128)}) fusion(bf16[256,2688]{1,0:T(8,128)(2,1)S(1)} %get-tuple-element.39.x_ref.bc_ref, f32[256,2560]{1,0:T(8,128)} %fusion.37, bf16[40,2560]{1,0:T(8,128)(2,1)S(1)} %copy-done.4, f32[256]{0:T(256)S(1)} %get-tuple-element.51, f32[40,256]{1,0:T(8,128)} %copy-done.7, ...), kind=kOutput, calls=%fused_computation.8 | convolution fusion | flops 55193600 | bytes 8131904 | tf_op jit(solution)/shard_map/dot_general | solution.py:33
  36.3 1.2 pad_maximum_fusion.1.parts_ref
  37.5 55.3 %core.1 = (bf16[256,2560]{1,0:T(8,128)(2,1)}, f32[20,4,256]{2,1,0:T(4,128)}, f32[20,1,128]{2,1,0:T(1,128)}, f32[256,128]{1,0:T(8,128)}, f32[64,2560]{1,0:T(8,128)}, /*index=5*/f32[64,2560]{1,0:T(8,128)}) custom-call(bf16[256,2688]{1,0:T(8,128)(2,1)} %copy-done, bf16[256,2560]{1,0:T(8,128)(2,1)} %bitcast.122, f32[20,8,256]{2,1,0:T(8,128)} %maximum_maximum_fusion.steps_ref, ...), custom_call_target="tpu_custom_call" | custom-call | tf_op jit(solution)/shard_map/core/pallas_call | solution.py:236
  93.5 18.8 %finish.1 = (bf16[256,2688]{1,0:T(8,128)(2,1)}, bf16[8,2688]{1,0:T(8,128)(2,1)}, f32[8,2688]{1,0:T(8,128)}, f32[20,4,256]{2,1,0:T(4,128)}, f32[20,1,128]{2,1,0:T(1,128)}) custom-call(bf16[256,2688]{1,0:T(8,128)(2,1)} %copy-done, f32[256,2688]{1,0:T(8,128)} %get-tuple-element.40.pre_ref, bf16[256,2688]{1,0:T(8,128)(2,1)} %bitcast.121, ...), custom_call_target="tpu_custom_call" | custom-call | tf_op jit(solution)/shard_map/finish/pallas_call | solution.py:342
  112.3 0.9 slice.114
  114.4 2.0 %collective-permute-start.1 = (bf16[3,2688]{1,0:T(4,128)(2,1)S(1)}, bf16[3,2688]{1,0:T(4,128)(2,1)S(1)}, u32[]{:S(2)}, u32[]{:S(2)}) collective-permute-start(bf16[3,2688]{1,0:T(4,128)(2,1)S(1)} %slice.114), channel_id=1, source_target_pairs={{16,0},{32,16},{48,32},{64,48},{80,64},{96,80},{112,96},{128,112},... | collective-permute-start | bytes 48392 | tf_op jit(solution)/shard_map/ppermute | solution.py:23
  116.6 1.1 slice_reduce_fusion.5
  117.9 1.2 fusion.48
  119.6 45.4 %total.1 = (f32[8,2688]{1,0:T(8,128)}, f32[8,128]{1,0:T(8,128)}) custom-call(f32[8,2688]{1,0:T(8,128)} %get-tuple-element.29.wide_ref, f32[8,128]{1,0:T(8,128)} %select_maximum_fusion.small_ref), custom_call_target="tpu_custom_call" | custom-call | tf_op jit(solution)/shard_map/total/pallas_call | solution.py:465
  165.1 1.3 slice_bitcast_fusion.1
  166.4 1.5 slice_reduce_fusion
  167.9 1.5 slice.119
  169.6 1.1 copy-done.6
  (103 shorter events, 10.2 us)
Async XLA Ops:
  0.6 16.4 %copy-start.4 = (bf16[40,2560]{1,0:T(8,128)(2,1)S(1)}, bf16[40,2560]{1,0:T(8,128)(2,1)}, u32[]{:S(2)}) copy-start(bf16[40,2560]{1,0:T(8,128)(2,1)} %constant.57) | copy-start | bytes 614404
  0.6 16.4 %copy-start.18 = (f32[40]{0:T(128)S(1)}, f32[40]{0:T(128)}, u32[]{:S(2)}) copy-start(f32[40]{0:T(128)} %param.14) | copy-start | bytes 484
  0.7 16.4 %copy-start.8 = (bf16[1,256,40]{1,2,0:T(8,128)(2,1)S(1)}, bf16[1,256,40]{1,2,0:T(8,128)(2,1)}, u32[]{:S(2)}) copy-start(bf16[1,256,40]{1,2,0:T(8,128)(2,1)} %param.11) | copy-start | bytes 61444
  1.5 22.2 %collective-permute-start = (bf16[3,2688]{1,0:T(4,128)(2,1)S(1)}, bf16[3,2688]{1,0:T(4,128)(2,1)S(1)}, u32[]{:S(2)}, u32[]{:S(2)}) collective-permute-start(bf16[3,2688]{1,0:T(4,128)(2,1)S(1)} %slice_bitcast_fusion), channel_id=1, source_target_pairs={{0,16},{16,32},{32,48},{48,64},{64,80},{80,96},{96,112},{112,128},... | collective-permute-start | bytes 48392 | tf_op jit(solution)/shard_map/ppermute | solution.py:23
  6.5 7.7 %copy-start.22 = (s32[256]{0:T(256)}, s32[256]{0:T(256)S(1)}, u32[]{:S(2)}) copy-start(s32[256]{0:T(256)S(1)} %iota_add_fusion) | copy-start | bytes 3076
  13.1 6.1 %copy-start.7 = (f32[40,256]{1,0:T(8,128)}, f32[40,256]{1,0:T(8,128)S(1)}, u32[]{:S(2)}) copy-start(f32[40,256]{1,0:T(8,128)S(1)} %fusion.5) | copy-start | bytes 122884
  15.4 3.8 %copy-start.3 = (bf16[1,256,2560]{2,1,0:T(8,128)(2,1)S(1)}, bf16[1,256,2560]{2,1,0:T(8,128)(2,1)}, u32[]{:S(2)}) copy-start(bf16[1,256,2560]{2,1,0:T(8,128)(2,1)} %param.17) | copy-start | bytes 3932164
  19.2 4.6 %copy-start.13 = (f32[2688]{0:T(1024)S(1)}, f32[2688]{0:T(1024)}, u32[]{:S(2)}) copy-start(f32[2688]{0:T(1024)} %param.13) | copy-start | bytes 32260
  19.8 11.2 %copy-start.2 = (bf16[256,2560]{1,0:T(8,128)(2,1)}, bf16[256,2560]{1,0:T(8,128)(2,1)S(1)}, u32[]{:S(2)}) copy-start(bf16[256,2560]{1,0:T(8,128)(2,1)S(1)} %fusion.1.led_ref) | copy-start | bytes 3932164
  21.3 9.7 %copy-start.15 = (s32[256]{0:T(256)}, s32[256]{0:T(256)S(1)}, u32[]{:S(2)}) copy-start(s32[256]{0:T(256)S(1)} %slice.96) | copy-start | bytes 3076
  23.8 7.2 %copy-start.10 = (bf16[3,2688]{1,0:T(4,128)(2,1)}, bf16[3,2688]{1,0:T(4,128)(2,1)S(1)}, u32[]{:S(2)}) copy-start(bf16[3,2688]{1,0:T(4,128)(2,1)S(1)} %collective-permute-done) | copy-start | bytes 48388
  31.0 4.6 %copy-start = (bf16[256,2688]{1,0:T(8,128)(2,1)}, bf16[256,2688]{1,0:T(8,128)(2,1)S(1)}, u32[]{:S(2)}) copy-start(bf16[256,2688]{1,0:T(8,128)(2,1)S(1)} %get-tuple-element.39.x_ref.bc_ref) | copy-start | bytes 4128772
  35.5 57.2 %copy-start.1 = (bf16[256,2560]{1,0:T(8,128)(2,1)}, bf16[256,2560]{1,0:T(8,128)(2,1)S(1)}, u32[]{:S(2)}) copy-start(bf16[256,2560]{1,0:T(8,128)(2,1)S(1)} %get-tuple-element.57.weighted_ref) | copy-start | bytes 3932164
  36.3 56.5 %copy-start.11 = (bf16[3,2688]{1,0:T(4,128)(2,1)S(1)}, bf16[3,2688]{1,0:T(4,128)(2,1)}, u32[]{:S(2)}) copy-start(bf16[3,2688]{1,0:T(4,128)(2,1)} %copy-done.10) | copy-start | bytes 48388
  93.4 20.5 %copy-start.14 = (f32[20,1,128]{2,1,0:T(1,128)S(1)}, f32[20,1,128]{2,1,0:T(1,128)}, u32[]{:S(2)}) copy-start(f32[20,1,128]{2,1,0:T(1,128)} %get-tuple-element.30) | copy-start | bytes 30724
  93.4 23.0 %copy-start.12 = (f32[20,4,256]{2,1,0:T(4,128)S(1)}, f32[20,4,256]{2,1,0:T(4,128)}, u32[]{:S(2)}) copy-start(f32[20,4,256]{2,1,0:T(4,128)} %get-tuple-element.26) | copy-start | bytes 245764
  93.4 24.4 %copy-start.17 = (f32[40,1]{0,1:T(1,128)S(1)}, f32[40,1]{0,1:T(1,128)}, u32[]{:S(2)}) copy-start(f32[40,1]{0,1:T(1,128)} %copy-done.16) | copy-start | bytes 484
  93.4 24.4 %copy-start.9 = (bf16[1,256,40]{1,2,0:T(8,128)(2,1)S(1)}, bf16[1,256,40]{1,2,0:T(8,128)(2,1)}, u32[]{:S(2)}) copy-start(bf16[1,256,40]{1,2,0:T(8,128)(2,1)} %param.11) | copy-start | bytes 61444
  93.5 24.4 %copy-start.19 = (f32[40]{0:T(128)S(1)}, f32[40]{0:T(128)}, u32[]{:S(2)}) copy-start(f32[40]{0:T(128)} %param.14) | copy-start | bytes 484
  93.5 24.4 %copy-start.23 = (s32[256]{0:T(256)S(1)}, s32[256]{0:T(256)}, u32[]{:S(2)}) copy-start(s32[256]{0:T(256)} %copy-done.22) | copy-start | bytes 3076
  93.5 24.4 %copy-start.25 = (f32[40]{0:T(128)S(1)}, f32[40]{0:T(128)}, u32[]{:S(2)}) copy-start(f32[40]{0:T(128)} %copy-done.24) | copy-start | bytes 484
  93.5 25.5 %copy-start.21 = (f32[40]{0:T(128)S(1)}, f32[40]{0:T(128)}, u32[]{:S(2)}) copy-start(f32[40]{0:T(128)} %param.15) | copy-start | bytes 484
  112.3 57.1 %copy-start.5 = (bf16[256,2688]{1,0:T(8,128)(2,1)S(1)}, bf16[256,2688]{1,0:T(8,128)(2,1)}, u32[]{:S(2)}) copy-start(bf16[256,2688]{1,0:T(8,128)(2,1)} %get-tuple-element.24) | copy-start | bytes 4128772
  114.4 55.2 %collective-permute-start.1 = (bf16[3,2688]{1,0:T(4,128)(2,1)S(1)}, bf16[3,2688]{1,0:T(4,128)(2,1)S(1)}, u32[]{:S(2)}, u32[]{:S(2)}) collective-permute-start(bf16[3,2688]{1,0:T(4,128)(2,1)S(1)} %slice.114), channel_id=1, source_target_pairs={{16,0},{32,16},{48,32},{64,48},{80,64},{96,80},{112,96},{128,112},... | collective-permute-start | bytes 48392 | tf_op jit(solution)/shard_map/ppermute | solution.py:23
  (4 other events, 8.2 us)
